TPU v7x, 32 devices: a whole 2x2x4 slice. The times are simulated.
32 devices in a mesh: group: 2 (over x), rep: 16 (over z, y, core).
Axes of the slice: x: 2, y: 2, z: 4, core: 2. Of those that a mesh axis runs over, the one named last changes fastest.
Arguments:
- queries: bfloat16 [4096, 4096], P(('group', 'rep')), parts along dimension 0
- prompt_keys: bfloat16 [4096, 512], P(('group', 'rep')), parts along dimension 0
- prompt_value_rows: bfloat16 [4096, 512], P(('group', 'rep')), parts along dimension 0, may hold values from -6 to 6
- document_keys: bfloat16 [16384, 512], P(('group', 'rep')), parts along dimension 0, may hold values from -12 to 12
- document_values: bfloat16 [16384, 512], P(('group', 'rep')), parts along dimension 0, may hold values from -6 to 6
- span_owner: int32 [32], P('group'), parts along dimension 0, may hold values from 0 to 15, each once
- block_list: int32 [32, 8], P(('group', 'rep')), parts along dimension 0, may hold values from 0 to 63, as said below
- prompt_length: int32 [32], P(('group', 'rep')), parts along dimension 0, may hold values from 2 to 128
Outputs:
- attended: bfloat16 [4096, 4096], P(('group', 'rep')), parts along dimension 0
There are 2 independent parts, one for each index of `group`. A program takes and returns all parts, laid end to end along the dimension named above; each array names one. Nothing has to cross between parts.
Inputs may be any that keep to these rules, and one draw needn't show every extreme that they name: Each replica holds exactly one span: span_owner is a permutation. `block_list`: the 8 blocks listed by one replica lie in 8 different spans.
All inputs are finite; a program needn't handle non-finite values.
Results may differ from a plain program's by a relative error of at most 0.0049.
Values may be sent and summed in bfloat16 or wider, within the bound.
No kernel may reach another device: no remote copies, remote signals or barrier semaphores. Data moves between devices by JAX's collectives and lax.ppermute only.
A program may use at most 128 MiB of HBM per device.

v0:
```python
import functools
import math

import jax
import jax.numpy as jnp
from jax import lax
from jax.experimental import pallas as pl
from jax.experimental.pallas import tpu as pltpu
from jax.sharding import PartitionSpec as P

QUERY_HEADS = 32
KEY_VALUE_HEADS = 4
HEAD_SIZE = 128
BLK = 128
SPAN_BLK = 4
LIST = 8
GROUP = QUERY_HEADS // KEY_VALUE_HEADS
HALF_HEADS = KEY_VALUE_HEADS // 2
HALF_KV = HALF_HEADS * HEAD_SIZE
HALF_Q = HALF_HEADS * GROUP * HEAD_SIZE
SCALE2 = math.log2(math.e) / math.sqrt(HEAD_SIZE)


SMEM = pl.BlockSpec(memory_space=pltpu.SMEM)
VMEM = pl.BlockSpec(memory_space=pltpu.VMEM)
ANY = pl.BlockSpec(memory_space=pl.ANY)


def rank_pairs(move):
    pairs = []
    for z in range(4):
        for y in range(2):
            for c in range(2):
                to = move(z, y, c)
                if to is not None:
                    pairs.append((z * 4 + y * 2 + c, to[0] * 4 + to[1] * 2 + to[2]))
    return pairs


CORE = rank_pairs(lambda z, y, c: (z, y, 1 - c))
SIDE = rank_pairs(lambda z, y, c: (z, 1 - y, c))
MID_SIDE = rank_pairs(lambda z, y, c: (z, 1 - y, c) if z in (1, 2) else None)
OUTER = rank_pairs(lambda z, y, c: (z ^ 1, y, c))
INNER = rank_pairs(lambda z, y, c: (3 - z, y, c) if z in (1, 2) else None)
END = rank_pairs(lambda z, y, c: (z ^ 1, y, c) if z in (1, 2) else None)
END_SIDE = rank_pairs(lambda z, y, c: (z ^ 1, 1 - y, c) if z in (1, 2) else None)


def hop(x, pairs):
    return lax.ppermute(x, "rep", pairs)


def place():
    rank = lax.axis_index("rep")
    return rank // 4, (rank // 2) % 2, rank % 2


def slot_kernel(plane_of, dests, rels, owner_ref, *refs):
    lists, refs = refs[:dests], refs[dests:]
    spans, refs = refs[: len(rels)], refs[len(rels) + 1 :]
    outs, sems = refs[:dests], refs[dests]
    z, y, c = place()
    copies = []
    for t in range(dests):
        for d in range(2):
            at = [jnp.int32(0)] * len(rels)
            for j in range(LIST):
                block = lists[t][d, j]
                owner = owner_ref[block // SPAN_BLK]
                for k, rel in enumerate(rels):
                    rank = plane_of(z) * 4 + y * 2 + (1 - c if rel else c)
                    at[k] = jnp.where(owner == rank, block % SPAN_BLK, at[k])
            for k, source in enumerate(spans):
                spot = d * len(rels) + k
                copy = pltpu.make_async_copy(
                    source.at[at[k]], outs[t].at[spot], sems.at[t * 2 * len(rels) + spot]
                )
                copy.start()
                copies.append(copy)
    for copy in copies:
        copy.wait()


def slots(plane_of, owner, lists, spans, rels, after):
    dests = len(lists)
    count = 2 * len(rels)
    shape = jax.ShapeDtypeStruct((count, BLK, 2 * HALF_KV), jnp.bfloat16)
    size = dests * count * BLK * 2 * HALF_KV * 2
    return pl.pallas_call(
        functools.partial(slot_kernel, plane_of, dests, rels),
        out_shape=[shape] * dests,
        in_specs=[SMEM] * (1 + dests) + [ANY] * (len(rels) + 1),
        out_specs=[VMEM] * dests,
        scratch_shapes=[pltpu.SemaphoreType.DMA((count * dests,))],
        cost_estimate=pl.CostEstimate(flops=0, bytes_accessed=2 * size, transcendentals=0),
        compiler_params=pltpu.CompilerParams(vmem_limit_bytes=8 << 20),
    )(owner, *lists, *[spans[rel].reshape(SPAN_BLK, BLK, 2 * HALF_KV) for rel in rels], after)


def softmax_part(blocks, odd, prompt, held_of, query, s_ref, p_ref, state_in, state_out, out):
    pieces = blocks + (1 if prompt else 0)
    row = lax.broadcasted_iota(jnp.int32, (BLK, BLK), 0)
    col = lax.broadcasted_iota(jnp.int32, (BLK, BLK), 1)
    width = pieces * BLK
    s_ref[:, :width] = lax.dot_general(
        query, held_of(pieces, 0), (((1,), (1,)), ((), ())), preferred_element_type=jnp.float32
    )
    scales, tops, totals = [], [], []
    for h in range(GROUP):
        rows = slice(h * BLK, (h + 1) * BLK)
        parts = []
        for j in range(pieces):
            part = s_ref[rows, j * BLK : (j + 1) * BLK]
            if prompt and j == 0:
                part = jnp.where(col <= row, part, -jnp.inf)
            elif j == pieces - 1:
                part = jnp.where(odd, -jnp.inf, part)
            parts.append(part)
        top = functools.reduce(jnp.maximum, parts)
        top = jnp.max(top, axis=1, keepdims=True)
        if state_in is not None:
            before = state_in[1][:, h : h + 1]
            top = jnp.maximum(top, before)
            scale = jnp.exp2((before - top) * SCALE2)
            scales.append(scale)
        total = None
        for j, part in enumerate(parts):
            weight = jnp.exp2((part - top) * SCALE2)
            total = weight if total is None else total + weight
            p_ref[rows, j * BLK : (j + 1) * BLK] = weight.astype(jnp.bfloat16)
        total = jnp.sum(total, axis=1, keepdims=True)
        if state_in is not None:
            total = total + scale * state_in[1][:, GROUP + h : GROUP + h + 1]
        tops.append(top)
        totals.append(total)
    mixed = lax.dot_general(
        p_ref[:, :width],
        held_of(pieces, 1),
        (((1,), (0,)), ((), ())),
        preferred_element_type=jnp.float32,
    )
    stats = jnp.zeros((BLK, BLK), jnp.float32)
    for h in range(GROUP):
        rows = slice(h * BLK, (h + 1) * BLK)
        value = mixed[rows]
        if state_in is not None:
            value = value + scales[h] * state_in[0][rows]
        if out is not None:
            out(h, (value * (1.0 / totals[h])).astype(jnp.bfloat16))
        else:
            state_out[0][rows] = value
            stats = jnp.where(col == h, tops[h], stats)
            stats = jnp.where(col == GROUP + h, totals[h], stats)
    if out is None:
        state_out[1][...] = stats


def attend_kernel(levels, first, final, owner_ref, list_ref, *refs):
    refs = list(refs)
    if first:
        q_ref, pair_q_ref, kp_ref, vp_ref, pair_kv_ref = refs[:5]
        refs = refs[5:]
    else:
        stacked_ref, acc_ref, stats_ref = refs[:3]
        refs = refs[3:]
    table = source_table(levels)
    sources, refs = refs[: len(table)], refs[len(table) + 1 :]
    if first:
        stacked_ref = refs.pop(0)
    if final:
        out_ref = refs.pop(0)
    else:
        acc_out, stats_out = refs.pop(0), refs.pop(0)
    held, s_ref, p_ref, count_ref, sems = refs
    room = min(4 * len(levels), LIST)
    base = 1 if first else 0
    z, y, c = place()
    near = z ^ 1
    mid = jnp.logical_or(z == 1, z == 2)
    inner = jnp.where(mid, 3 - z, 3 - near)
    for d in range(2):

        def fetch(j, count, d=d):
            block = list_ref[d, j]
            owner = owner_ref[block // SPAN_BLK]
            oz, oy, oc = owner // 4, (owner // 2) % 2, owner % 2
            rel = (oc != c).astype(jnp.int32)
            level = jnp.where(oz == z, 0, jnp.where(oz == near, 1, jnp.where(oz == inner, 2, 3)))
            own_column = oy == y
            whole = jnp.logical_and(own_column, jnp.logical_or(level < 2, mid))
            spot_whole = block % SPAN_BLK
            listed = functools.reduce(jnp.logical_or, [level == one for one in levels])
            for (at_level, form, at_rel), source in zip(table, sources):
                if form == "whole":
                    match = jnp.logical_and(whole, rel == at_rel)
                    spot = spot_whole
                elif form == "side":
                    match = jnp.logical_and(~own_column, jnp.logical_or(level < 2, mid))
                    spot = d * 2 + rel
                else:
                    match = jnp.logical_and(
                        ~mid, own_column if form == "end" else ~own_column
                    )
                    match = jnp.logical_and(match, rel == at_rel)
                    spot = d
                match = jnp.logical_and(match, level == at_level)

                @pl.when(match)
                def _(source=source, spot=spot):
                    pltpu.make_async_copy(
                        source.at[spot], held.at[d, base + count], sems.at[d, count]
                    ).start()

            return count + listed.astype(jnp.int32)

        count_ref[d] = lax.fori_loop(0, LIST, fetch, jnp.int32(0))

    if first:
        for g in range(HALF_HEADS):
            for h in range(GROUP):
                at = (g * GROUP + h) * HEAD_SIZE
                start = pl.multiple_of(c * HALF_Q + at, HEAD_SIZE)
                rows = slice(h * BLK, (h + 1) * BLK)
                stacked_ref[g, rows] = q_ref[:, pl.ds(start, HEAD_SIZE)]
                stacked_ref[HALF_HEADS + g, rows] = pair_q_ref[:, at : at + HEAD_SIZE]
        off = pl.multiple_of(c * HALF_KV, HALF_KV)
        held[0, 0, :, :HALF_KV] = kp_ref[:, pl.ds(off, HALF_KV)]
        held[0, 0, :, HALF_KV:] = vp_ref[:, pl.ds(off, HALF_KV)]
        held[1, 0] = pair_kv_ref[...]

    def part(i, carry):
        d, g = i // HALF_HEADS, i % HALF_HEADS
        count = count_ref[d]

        @pl.when(g == 0)
        def _():
            def arrive(j, carry):
                pltpu.make_async_copy(sources[0].at[0], held.at[d, base + j], sems.at[d, j]).wait()
                return carry

            lax.fori_loop(0, count, arrive, 0)

            @pl.when(count % 2 == 1)
            def _():
                held[d, base + count] = jnp.zeros((BLK, 2 * HALF_KV), jnp.bfloat16)

        def held_of(pieces, which):
            at = pl.multiple_of(which * HALF_KV + g * HEAD_SIZE, HEAD_SIZE)
            return held[d, :pieces, :, pl.ds(at, HEAD_SIZE)].reshape(pieces * BLK, HEAD_SIZE)

        out = None
        if final:

            def out(h, value):
                at = pl.multiple_of((g * GROUP + h) * HEAD_SIZE, HEAD_SIZE)
                out_ref[d, :, pl.ds(at, HEAD_SIZE)] = value

        for even in range(0, room + 1, 2):

            @pl.when((count + 1) // 2 * 2 == even)
            def _(even=even):
                if even == 0 and not first:
                    if final:
                        for h in range(GROUP):
                            value = acc_ref[i, h * BLK : (h + 1) * BLK, :]
                            total = stats_ref[i, :, GROUP + h : GROUP + h + 1]
                            out(h, (value * (1.0 / total)).astype(jnp.bfloat16))
                    else:
                        acc_out[i] = acc_ref[i]
                        stats_out[i] = stats_ref[i]
                    return
                softmax_part(
                    even,
                    count % 2 == 1,
                    first,
                    held_of,
                    stacked_ref[i],
                    s_ref,
                    p_ref,
                    None if first else (acc_ref.at[i], stats_ref.at[i]),
                    None if final else (acc_out.at[i], stats_out.at[i]),
                    out,
                )

        return carry

    lax.fori_loop(0, 2 * HALF_HEADS, part, 0)


def source_table(levels):
    table = []
    for level in levels:
        table += [(level, "whole", 0), (level, "whole", 1), (level, "side", None)]
        if level > 1:
            table += [(level, form, rel) for form in ("end", "end_side") for rel in range(2)]
    return table


def attend(levels, first, final, owner, lists, operands, sources, after):
    parts = 2 * HALF_HEADS
    room = min(4 * len(levels), LIST)
    pieces = room + (1 if first else 0)
    rows = GROUP * BLK
    stacked = jax.ShapeDtypeStruct((parts, rows, HEAD_SIZE), jnp.bfloat16)
    acc = jax.ShapeDtypeStruct((parts, rows, HEAD_SIZE), jnp.float32)
    stats = jax.ShapeDtypeStruct((parts, BLK, BLK), jnp.float32)
    outs = [stacked] if first else []
    outs += [jax.ShapeDtypeStruct((2, BLK, HALF_Q), jnp.bfloat16)] if final else [acc, stats]
    used = sources_of(levels, sources)
    keys = (pieces + 1) // 2 * BLK
    return pl.pallas_call(
        functools.partial(attend_kernel, levels, first, final),
        out_shape=outs,
        in_specs=[SMEM] * 2 + [VMEM] * len(operands) + [ANY] * (len(used) + 1),
        out_specs=[VMEM] * len(outs),
        scratch_shapes=[
            pltpu.VMEM((2, room + 1, BLK, 2 * HALF_KV), jnp.bfloat16),
            pltpu.VMEM((rows, pieces * BLK), jnp.float32),
            pltpu.VMEM((rows, pieces * BLK), jnp.bfloat16),
            pltpu.SMEM((2,), jnp.int32),
            pltpu.SemaphoreType.DMA((2, room)),
        ],
        cost_estimate=pl.CostEstimate(
            flops=4 * QUERY_HEADS * BLK * keys * HEAD_SIZE,
            bytes_accessed=4 << 20,
            transcendentals=QUERY_HEADS * BLK * keys,
        ),
        compiler_params=pltpu.CompilerParams(vmem_limit_bytes=30 << 20),
    )(owner, lists, *operands, *used, after)


def sources_of(levels, sources):
    return [sources[key].reshape(-1, BLK, 2 * HALF_KV) for key in source_table(levels)]


def line_device(
    queries,
    prompt_keys,
    prompt_value_rows,
    document_keys,
    document_values,
    span_owner,
    block_list,
    prompt_length,
):
    first = lax.axis_index("rep") % 2 == 0

    def half(x, mine):
        width = x.shape[1] // 2
        return jnp.where(first == mine, x[:, :width], x[:, width:])

    def paired(keys, values, mine):
        return jnp.concatenate([half(keys, mine), half(values, mine)], axis=1)

    own = [paired(document_keys, document_values, True)]
    own.append(hop(paired(document_keys, document_values, False), CORE))
    outer = [hop(own[rel], OUTER) for rel in range(2)]
    inner = [hop(own[rel], INNER) for rel in range(2)]
    far = [hop(outer[rel], INNER) for rel in range(2)]

    ahead = hop(block_list, OUTER)
    both = jnp.concatenate([block_list, ahead], axis=0)
    across = hop(both, CORE)
    four = jnp.concatenate([both, across], axis=0)
    beside = hop(four, SIDE)

    def chip_lists(four, at):
        return jnp.concatenate([four[at : at + 1], four[at + 2 : at + 3]], axis=0)

    lists, side_lists = chip_lists(four, 0), chip_lists(beside, 0)
    near_lists = [chip_lists(four, 1), chip_lists(beside, 1)]
    pair_q = hop(half(queries, False), CORE)
    pair_kv = hop(paired(prompt_keys, prompt_value_rows, False), CORE)

    planes = [lambda z: z, lambda z: z ^ 1, lambda z: 3 - z, lambda z: (3 - z) ^ 1]
    spans = (own, outer, inner, far)
    sources = {(level, "whole", rel): spans[level][rel] for level in range(4) for rel in range(2)}

    def send_side(level, after):
        (side,) = slots(planes[level], span_owner, [side_lists], spans[level], (0, 1), after)
        sources[level, "side", None] = hop(side, SIDE if level < 2 else MID_SIDE)
        return side

    def send_end(level, rel, after):
        end, end_side = slots(planes[level], span_owner, near_lists, spans[level], (rel,), after)
        sources[level, "end", rel] = hop(end, END)
        sources[level, "end_side", rel] = hop(end_side, END_SIDE)
        return end

    last = send_side(0, own[0])
    last = send_end(2, 0, last)
    last = send_side(1, last)
    last = send_end(2, 1, last)
    last = send_side(2, last)
    last = send_end(3, 0, last)
    last = send_end(3, 1, last)
    last = send_side(3, last)
    operands = [queries, pair_q, prompt_keys, prompt_value_rows, pair_kv]
    operands = attend((0, 1, 2), True, False, span_owner, lists, operands, sources, last)
    (halves,) = attend((3,), False, True, span_owner, lists, operands, sources, last)
    mine, theirs = halves[0], hop(halves[1], CORE)
    joined = jnp.where(
        first,
        jnp.concatenate([mine, theirs], axis=1),
        jnp.concatenate([theirs, mine], axis=1),
    )
    live = jnp.arange(BLK, dtype=jnp.int32) < prompt_length[0]
    return jnp.where(live[:, None], joined, jnp.zeros_like(joined))


def probs_of(query_part, key_part, visible):
    scores = jnp.einsum(
        "thd,kd->htk", query_part, key_part, preferred_element_type=jnp.float32
    ) * query_part.shape[-1] ** (-0.5)
    scores = jnp.where(visible[None], scores, -jnp.inf)
    largest = jnp.max(scores, axis=-1, keepdims=True)
    weights = jnp.exp(scores - largest)
    return (weights / jnp.sum(weights, axis=-1, keepdims=True)).astype(jnp.bfloat16)


def per_device(
    queries,
    prompt_keys,
    prompt_value_rows,
    document_keys,
    document_values,
    span_owner,
    block_list,
    prompt_length,
):
    group_width = QUERY_HEADS // KEY_VALUE_HEADS
    count = lax.axis_size("rep")
    list_len = block_list.shape[1]
    all_ranks = jnp.arange(count, dtype=jnp.int32)
    my_list = block_list[0]
    list_span = my_list // SPAN_BLK
    owners = jnp.sum(
        jnp.where(list_span[:, None] == all_ranks[None, :], span_owner[None, :], 0), axis=1
    )
    matches = owners[None, :] == all_ranks[:, None]
    request = jnp.sum(jnp.where(matches, (my_list % SPAN_BLK + 1)[None, :], 0), axis=1) - 1
    arrived = lax.all_to_all(request, "rep", split_axis=0, concat_axis=0, tiled=True)
    wanted = arrived >= 0
    inner_block = jnp.maximum(arrived, 0)

    def outgoing(source):
        blocks = source.reshape(SPAN_BLK, BLK, source.shape[1])
        picked = jnp.take(blocks, inner_block, axis=0)
        return jnp.where(wanted[:, None, None], picked, jnp.zeros_like(picked))

    def listed(received):
        return jnp.take(received, owners, axis=0).reshape(list_len * BLK, received.shape[2])

    send_keys = outgoing(document_keys)
    send_values = outgoing(document_values)
    doc_visible = jnp.ones((BLK, list_len * BLK), dtype=bool)
    got_keys, got_values = (
        lax.all_to_all(send_keys, "rep", split_axis=0, concat_axis=0, tiled=True),
        lax.all_to_all(send_values, "rep", split_axis=0, concat_axis=0, tiled=True),
    )
    query_block = 0
    seen = (query_block + 1) * BLK
    key_rows = jnp.concatenate([listed(got_keys), prompt_keys], axis=0)
    slots = jnp.arange(seen, dtype=jnp.int32)
    positions = query_block * BLK + jnp.arange(BLK, dtype=jnp.int32)
    visible = jnp.concatenate([doc_visible, slots[None, :] <= positions[:, None]], axis=1)
    row_probs = []
    for all_head_cluster in range(KEY_VALUE_HEADS):
        cols = slice(
            all_head_cluster * group_width * HEAD_SIZE,
            (all_head_cluster + 1) * group_width * HEAD_SIZE,
        )
        query_part = queries[query_block * BLK : seen, cols].reshape(BLK, group_width, HEAD_SIZE)
        row_probs.append(
            probs_of(
                query_part,
                key_rows[:, all_head_cluster * HEAD_SIZE : (all_head_cluster + 1) * HEAD_SIZE],
                visible,
            )
        )
    table = [row_probs]
    doc_value_rows = listed(got_values)
    live_rows = prompt_length[0]
    query_block = 0
    value_rows = jnp.concatenate([doc_value_rows, prompt_value_rows], axis=0)
    pieces = []
    for head_cluster in range(KEY_VALUE_HEADS):
        mixed = jnp.einsum(
            "htk,kd->thd",
            table[query_block][head_cluster],
            value_rows[:, head_cluster * HEAD_SIZE : (head_cluster + 1) * HEAD_SIZE],
            preferred_element_type=jnp.float32,
        )
        pieces.append(mixed.reshape(BLK, group_width * HEAD_SIZE))
    joined = jnp.concatenate(pieces, axis=1).astype(jnp.bfloat16)
    positions = query_block * BLK + jnp.arange(BLK, dtype=jnp.int32)
    outputs = jnp.where((positions < live_rows)[:, None], joined, jnp.zeros_like(joined))
    return outputs


def layered(*args):
    return line_device(*args)


def solution(mesh):
    line = mesh.shape["rep"] == 16
    return jax.shard_map(
        layered if line else per_device,
        mesh=mesh,
        in_specs=(
            P(("group", "rep"), None),
            P(("group", "rep"), None),
            P(("group", "rep"), None),
            P(("group", "rep"), None),
            P(("group", "rep"), None),
            P("group"),
            P(("group", "rep"), None),
            P(("group", "rep")),
        ),
        out_specs=P(("group", "rep"), None),
        check_vma=False,
    )
```

profile of v0, /device:TPU:15, one launch (start us, length us, event | category | flops | bytes accessed | tf_op | source)
XLA Modules:
  0.0 114.3 jit_solution(3578747391879248338)
XLA Ops:
  0.0 1.3 %broadcast_select_fusion = (bf16[512,256]{1,0:T(8,128)(2,1)S(1)}, bf16[512,256]{1,0:T(8,128)(2,1)S(1)}, bf16[512,256]{1,0:T(8,128)(2,1)S(1)}, bf16[512,256]{1,0:T(8,128)(2,1)S(1)}) fusion(pred[]{:T(512)S(6)} %eq.7, bf16[512,512]{1,0:T(8,128)(2,1)} %param.12, pred[]{:T(512)S(6)} %eq.6, bf16[512,512]{1,0:T(8,128)(2,1)} %param.11), kind=kLoop, calls=%fused_computation.7 | loop fusion | flops 524288 | bytes 2097154 | tf_op jit(solution)/shard_map/jit(_where)/select_n | solution.py:350
  1.4 3.3 %collective-permute-start.9 = (bf16[512,512]{1,0:T(8,128)(2,1)S(1)}, bf16[512,512]{1,0:T(8,128)(2,1)S(1)}, u32[]{:S(2)}, u32[]{:S(2)}) collective-permute-start(bf16[512,512]{1,0:T(8,128)(2,1)S(1)} %pad_maximum_fusion.refs_3_), channel_id=1, source_target_pairs={{4,8},{5,9},{6,10},{7,11},{8,4},{9,5},{10,6},{11,7},{20,24},{21,25... | collective-permute-start | bytes 1572872 | tf_op jit(solution)/shard_map/ppermute | solution.py:50
  5.9 1.7 %collective-permute-start = (s32[1,8]{1,0:T(1,128)S(1)}, s32[1,8]{1,0:T(1,128)S(1)}, u32[]{:S(2)}, u32[]{:S(2)}) collective-permute-start(s32[1,8]{1,0:T(1,128)S(1)} %copy-done.4), channel_id=1, source_target_pairs={{0,4},{1,5},{2,6},{3,7},{4,0},{5,1},{6,2},{7,3},{8,12},{9,13},{10,... | collective-permute-start | bytes 104 | tf_op jit(solution)/shard_map/ppermute | solution.py:50
  8.2 9.2 %collective-permute-done = s32[1,8]{1,0:T(1,128)S(1)} collective-permute-done((s32[1,8]{1,0:T(1,128)S(1)}, s32[1,8]{1,0:T(1,128)S(1)}, u32[]{:S(2)}, u32[]{:S(2)}) %collective-permute-start) | collective-permute-done | bytes 64 | tf_op jit(solution)/shard_map/ppermute | solution.py:50
  17.4 2.0 %collective-permute-start.1 = (s32[2,8]{1,0:T(2,128)S(1)}, s32[2,8]{1,0:T(2,128)S(1)}, u32[]{:S(2)}, u32[]{:S(2)}) collective-permute-start(s32[2,8]{1,0:T(2,128)S(1)} %pad_add_fusion.1), channel_id=1, source_target_pairs={{0,1},{1,0},{2,3},{3,2},{4,5},{5,4},{6,7},{7,6},{8,9},{9,8},{10,11... | collective-permute-start | bytes 200 | tf_op jit(solution)/shard_map/ppermute | solution.py:50
  20.5 2.2 %collective-permute-done.5 = s32[4,8]{1,0:T(4,128)S(1)} collective-permute-done((s32[4,8]{1,0:T(4,128)S(1)}, s32[4,8]{1,0:T(4,128)S(1)}, u32[]{:S(2)}, u32[]{:S(2)}) %collective-permute-start.5) | collective-permute-done | bytes 160 | tf_op jit(solution)/shard_map/ppermute | solution.py:50
  22.7 2.1 %collective-permute-start.11 = (bf16[512,512]{1,0:T(8,128)(2,1)S(1)}, bf16[512,512]{1,0:T(8,128)(2,1)S(1)}, u32[]{:S(2)}, u32[]{:S(2)}) collective-permute-start(bf16[512,512]{1,0:T(8,128)(2,1)S(1)} %collective-permute-done.4), channel_id=1, source_target_pairs={{4,8},{5,9},{6,10},{7,11},{8,4},{9,5},{10,6},{11,7},{20,24},{21,25... | collective-permute-start | bytes 1572872 | tf_op jit(solution)/shard_map/ppermute | solution.py:50
  24.8 1.8 %collective-permute-start.3 = (bf16[128,512]{1,0:T(8,128)(2,1)S(1)}, bf16[128,512]{1,0:T(8,128)(2,1)S(1)}, u32[]{:S(2)}, u32[]{:S(2)}) collective-permute-start(bf16[128,512]{1,0:T(8,128)(2,1)S(1)} %pad_maximum_fusion.2), channel_id=1, source_target_pairs={{0,1},{1,0},{2,3},{3,2},{4,5},{5,4},{6,7},{7,6},{8,9},{9,8},{10,11... | collective-permute-start | bytes 393224 | tf_op jit(solution)/shard_map/ppermute | solution.py:50
  26.7 1.4 %shard_map.82.refs_3_ = bf16[4,128,512]{2,1,0:T(8,128)(2,1)S(1)} custom-call(s32[16]{0:T(128)S(1)} %copy-done.3, s32[2,8]{1,0:T(2,128)S(1)} %pad_add_fusion.3.refs_0_, bf16[4,128,512]{2,1,0:T(8,128)(2,1)S(1)} %bitcast.14, bf16[4,128,512]{2,1,0:T(8,128)(2,1)S(1)} %bitcast.30, bf16[512,512]{1,0:T(8,128)(2,1)S(1)} %pad_maximum_fusion.refs_3_), custom_call_target="tpu_custom_call" | custom-call | bytes 1048576 | tf_op jit(solution)/shard_map/pallas_call | solution.py:89
  28.1 3.2 %collective-permute-start.17 = (bf16[512,512]{1,0:T(8,128)(2,1)S(1)}, bf16[512,512]{1,0:T(8,128)(2,1)S(1)}, u32[]{:S(2)}, u32[]{:S(2)}) collective-permute-start(bf16[512,512]{1,0:T(8,128)(2,1)S(1)} %collective-permute-done.7), channel_id=1, source_target_pairs={{4,8},{5,9},{6,10},{7,11},{8,4},{9,5},{10,6},{11,7},{20,24},{21,25... | collective-permute-start | bytes 1572872 | tf_op jit(solution)/shard_map/ppermute | solution.py:50
  31.3 2.0 %collective-permute-done.8 = bf16[512,512]{1,0:T(8,128)(2,1)S(1)} collective-permute-done((bf16[512,512]{1,0:T(8,128)(2,1)S(1)}, bf16[512,512]{1,0:T(8,128)(2,1)S(1)}, u32[]{:S(2)}, u32[]{:S(2)}) %collective-permute-start.8) | collective-permute-done | bytes 524320 | tf_op jit(solution)/shard_map/ppermute | solution.py:50
  33.3 2.1 %collective-permute-start.18 = (bf16[512,512]{1,0:T(8,128)(2,1)S(1)}, bf16[512,512]{1,0:T(8,128)(2,1)S(1)}, u32[]{:S(2)}, u32[]{:S(2)}) collective-permute-start(bf16[512,512]{1,0:T(8,128)(2,1)S(1)} %collective-permute-done.8), channel_id=1, source_target_pairs={{4,8},{5,9},{6,10},{7,11},{8,4},{9,5},{10,6},{11,7},{20,24},{21,25... | collective-permute-start | bytes 1572872 | tf_op jit(solution)/shard_map/ppermute | solution.py:50
  35.4 1.5 %shard_map.83 = (bf16[2,128,512]{2,1,0:T(8,128)(2,1)S(1)}, bf16[2,128,512]{2,1,0:T(8,128)(2,1)S(1)}) custom-call(s32[16]{0:T(128)S(1)} %copy-done.3, s32[2,8]{1,0:T(2,128)S(1)} %pad_add_fusion.4.refs_0_, s32[2,8]{1,0:T(2,128)S(1)} %pad_add_fusion.5.refs_1_, bf16[4,128,512]{2,1,0:T(8,128)(2,1)S(1)} %bitcast.19, bf16[4,128,512]{2,1,0:T(8,128)(2,1)S(1)} %shard_map.82.refs_3_), custom_call_target="tpu_custom_call" | custom-call | bytes 1048576 | tf_op jit(solution)/shard_map/pallas_call | solution.py:89
  38.3 1.5 %collective-permute-start.15 = (bf16[2,128,512]{2,1,0:T(8,128)(2,1)S(1)}, bf16[2,128,512]{2,1,0:T(8,128)(2,1)S(1)}, u32[]{:S(2)}, u32[]{:S(2)}) collective-permute-start(bf16[2,128,512]{2,1,0:T(8,128)(2,1)S(1)} %get-tuple-element.18), channel_id=1, source_target_pairs={{4,2},{5,3},{6,0},{7,1},{8,14},{9,15},{10,12},{11,13},{20,18},{21,... | collective-permute-start | bytes 786440 | tf_op jit(solution)/shard_map/ppermute | solution.py:50
  40.9 1.4 %shard_map.84.refs_3_ = bf16[4,128,512]{2,1,0:T(8,128)(2,1)S(1)} custom-call(s32[16]{0:T(128)S(1)} %copy-done.3, s32[2,8]{1,0:T(2,128)S(1)} %pad_add_fusion.3.refs_0_, bf16[4,128,512]{2,1,0:T(8,128)(2,1)S(1)} %bitcast.28, bf16[4,128,512]{2,1,0:T(8,128)(2,1)S(1)} %bitcast.32, bf16[2,128,512]{2,1,0:T(8,128)(2,1)S(1)} %get-tuple-element.16.refs_3_), custom_call_target="tpu_custom_call" | custom-call | bytes 1048576 | tf_op jit(solution)/shard_map/pallas_call | solution.py:89
  42.3 1.5 %shard_map.85 = (bf16[2,128,512]{2,1,0:T(8,128)(2,1)S(1)}, bf16[2,128,512]{2,1,0:T(8,128)(2,1)S(1)}) custom-call(s32[16]{0:T(128)S(1)} %copy-done.3, s32[2,8]{1,0:T(2,128)S(1)} %pad_add_fusion.4.refs_0_, s32[2,8]{1,0:T(2,128)S(1)} %pad_add_fusion.5.refs_1_, bf16[4,128,512]{2,1,0:T(8,128)(2,1)S(1)} %bitcast.22, bf16[4,128,512]{2,1,0:T(8,128)(2,1)S(1)} %shard_map.84.refs_3_), custom_call_target="tpu_custom_call" | custom-call | bytes 1048576 | tf_op jit(solution)/shard_map/pallas_call | solution.py:89
  43.8 1.4 %shard_map.86.refs_3_ = bf16[4,128,512]{2,1,0:T(8,128)(2,1)S(1)} custom-call(s32[16]{0:T(128)S(1)} %copy-done.3, s32[2,8]{1,0:T(2,128)S(1)} %pad_add_fusion.3.refs_0_, bf16[4,128,512]{2,1,0:T(8,128)(2,1)S(1)} %bitcast.20, bf16[4,128,512]{2,1,0:T(8,128)(2,1)S(1)} %bitcast.23, bf16[2,128,512]{2,1,0:T(8,128)(2,1)S(1)} %get-tuple-element.17.refs_3_), custom_call_target="tpu_custom_call" | custom-call | bytes 1048576 | tf_op jit(solution)/shard_map/pallas_call | solution.py:89
  45.2 2.3 %collective-permute-start.12 = (bf16[4,128,512]{2,1,0:T(8,128)(2,1)S(1)}, bf16[4,128,512]{2,1,0:T(8,128)(2,1)S(1)}, u32[]{:S(2)}, u32[]{:S(2)}) collective-permute-start(bf16[4,128,512]{2,1,0:T(8,128)(2,1)S(1)} %shard_map.86.refs_3_), channel_id=1, source_target_pairs={{4,6},{5,7},{6,4},{7,5},{8,10},{9,11},{10,8},{11,9},{20,22},{21,23... | collective-permute-start | bytes 1572872 | tf_op jit(solution)/shard_map/ppermute | solution.py:50
  49.3 4.1 %collective-permute-start.14 = (bf16[2,128,512]{2,1,0:T(8,128)(2,1)S(1)}, bf16[2,128,512]{2,1,0:T(8,128)(2,1)S(1)}, u32[]{:S(2)}, u32[]{:S(2)}) collective-permute-start(bf16[2,128,512]{2,1,0:T(8,128)(2,1)S(1)} %get-tuple-element.17.refs_3_), channel_id=1, source_target_pairs={{4,0},{5,1},{6,2},{7,3},{8,12},{9,13},{10,14},{11,15},{20,16},{21,... | collective-permute-start | bytes 786440 | tf_op jit(solution)/shard_map/ppermute | solution.py:50
  53.4 5.6 %collective-permute-done.18 = bf16[512,512]{1,0:T(8,128)(2,1)S(1)} collective-permute-done((bf16[512,512]{1,0:T(8,128)(2,1)S(1)}, bf16[512,512]{1,0:T(8,128)(2,1)S(1)}, u32[]{:S(2)}, u32[]{:S(2)}) %collective-permute-start.18) | collective-permute-done | bytes 524320 | tf_op jit(solution)/shard_map/ppermute | solution.py:50
  60.3 1.5 %shard_map.87 = (bf16[2,128,512]{2,1,0:T(8,128)(2,1)S(1)}, bf16[2,128,512]{2,1,0:T(8,128)(2,1)S(1)}) custom-call(s32[16]{0:T(128)S(1)} %copy-done.3, s32[2,8]{1,0:T(2,128)S(1)} %pad_add_fusion.4.refs_0_, s32[2,8]{1,0:T(2,128)S(1)} %pad_add_fusion.5.refs_1_, bf16[4,128,512]{2,1,0:T(8,128)(2,1)S(1)} %bitcast.25, bf16[4,128,512]{2,1,0:T(8,128)(2,1)S(1)} %shard_map.86.refs_3_), custom_call_target="tpu_custom_call" | custom-call | bytes 1048576 | tf_op jit(solution)/shard_map/pallas_call | solution.py:89
  61.8 1.5 %shard_map.88 = (bf16[2,128,512]{2,1,0:T(8,128)(2,1)S(1)}, bf16[2,128,512]{2,1,0:T(8,128)(2,1)S(1)}) custom-call(s32[16]{0:T(128)S(1)} %copy-done.3, s32[2,8]{1,0:T(2,128)S(1)} %pad_add_fusion.4.refs_0_, s32[2,8]{1,0:T(2,128)S(1)} %pad_add_fusion.5.refs_1_, bf16[4,128,512]{2,1,0:T(8,128)(2,1)S(1)} %bitcast.16, bf16[2,128,512]{2,1,0:T(8,128)(2,1)S(1)} %get-tuple-element.20.refs_3_), custom_call_target="tpu_custom_call" | custom-call | bytes 1048576 | tf_op jit(solution)/shard_map/pallas_call | solution.py:89
  63.4 1.4 %shard_map.89.refs_18_.refs_10_ = bf16[4,128,512]{2,1,0:T(8,128)(2,1)S(1)} custom-call(s32[16]{0:T(128)S(1)} %copy-done.3, s32[2,8]{1,0:T(2,128)S(1)} %pad_add_fusion.3.refs_0_, bf16[4,128,512]{2,1,0:T(8,128)(2,1)S(1)} %bitcast.26, bf16[4,128,512]{2,1,0:T(8,128)(2,1)S(1)} %bitcast.17, bf16[2,128,512]{2,1,0:T(8,128)(2,1)S(1)} %get-tuple-element.21.refs_3_), custom_call_target="tpu_custom_call" | custom-call | bytes 1048576 | tf_op jit(solution)/shard_map/pallas_call | solution.py:89
  64.8 2.1 %collective-permute-start.19 = (bf16[4,128,512]{2,1,0:T(8,128)(2,1)S(1)}, bf16[4,128,512]{2,1,0:T(8,128)(2,1)S(1)}, u32[]{:S(2)}, u32[]{:S(2)}) collective-permute-start(bf16[4,128,512]{2,1,0:T(8,128)(2,1)S(1)} %shard_map.89.refs_18_.refs_10_), channel_id=1, source_target_pairs={{4,6},{5,7},{6,4},{7,5},{8,10},{9,11},{10,8},{11,9},{20,22},{21,23... | collective-permute-start | bytes 1572872 | tf_op jit(solution)/shard_map/ppermute | solution.py:50
  66.9 1.3 %collective-permute-start.20 = (bf16[2,128,512]{2,1,0:T(8,128)(2,1)S(1)}, bf16[2,128,512]{2,1,0:T(8,128)(2,1)S(1)}, u32[]{:S(2)}, u32[]{:S(2)}) collective-permute-start(bf16[2,128,512]{2,1,0:T(8,128)(2,1)S(1)} %get-tuple-element.20.refs_3_), channel_id=1, source_target_pairs={{4,0},{5,1},{6,2},{7,3},{8,12},{9,13},{10,14},{11,15},{20,16},{21,... | collective-permute-start | bytes 786440 | tf_op jit(solution)/shard_map/ppermute | solution.py:50
  69.6 1.3 %collective-permute-start.21 = (bf16[2,128,512]{2,1,0:T(8,128)(2,1)S(1)}, bf16[2,128,512]{2,1,0:T(8,128)(2,1)S(1)}, u32[]{:S(2)}, u32[]{:S(2)}) collective-permute-start(bf16[2,128,512]{2,1,0:T(8,128)(2,1)S(1)} %get-tuple-element.21.refs_3_), channel_id=1, source_target_pairs={{4,0},{5,1},{6,2},{7,3},{8,12},{9,13},{10,14},{11,15},{20,16},{21,... | collective-permute-start | bytes 786440 | tf_op jit(solution)/shard_map/ppermute | solution.py:50
  70.9 3.1 %collective-permute-done.10.refs_10_ = bf16[4,128,512]{2,1,0:T(8,128)(2,1)S(1)} collective-permute-done((bf16[4,128,512]{2,1,0:T(8,128)(2,1)S(1)}, bf16[4,128,512]{2,1,0:T(8,128)(2,1)S(1)}, u32[]{:S(2)}, u32[]{:S(2)}) %collective-permute-start.10) | collective-permute-done | bytes 524320 | tf_op jit(solution)/shard_map/ppermute | solution.py:50
  74.0 1.7 %collective-permute-start.23 = (bf16[2,128,512]{2,1,0:T(8,128)(2,1)S(1)}, bf16[2,128,512]{2,1,0:T(8,128)(2,1)S(1)}, u32[]{:S(2)}, u32[]{:S(2)}) collective-permute-start(bf16[2,128,512]{2,1,0:T(8,128)(2,1)S(1)} %get-tuple-element.26), channel_id=1, source_target_pairs={{4,2},{5,3},{6,0},{7,1},{8,14},{9,15},{10,12},{11,13},{20,18},{21,... | collective-permute-start | bytes 786440 | tf_op jit(solution)/shard_map/ppermute | solution.py:50
  75.8 18.7 %shard_map.90 = (bf16[4,1024,128]{2,1,0:T(8,128)(2,1)S(1)}, f32[4,1024,128]{2,1,0:T(8,128)S(1)}, f32[4,128,128]{2,1,0:T(8,128)S(1)}) custom-call(s32[16]{0:T(128)S(1)} %copy-done.3, s32[2,8]{1,0:T(2,128)S(1)} %pad_add_fusion.2.list_ref, bf16[128,4096]{1,0:T(8,128)(2,1)S(1)} %copy-done, bf16[128,2048]{1,0:T(8,128)(2,1)S(1)} %collective-permute-done.2.refs_1_, ...), custom_call_target="tpu_custom_call" | custom-call | flops 1342177280 | bytes 4194304 | tf_op jit(solution)/shard_map/pallas_call | solution.py:311
  94.5 12.2 %shard_map.91 = bf16[2,128,2048]{2,1,0:T(8,128)(2,1)S(1)} custom-call(s32[16]{0:T(128)S(1)} %copy-done.3, s32[2,8]{1,0:T(2,128)S(1)} %pad_add_fusion.2.list_ref, bf16[4,1024,128]{2,1,0:T(8,128)(2,1)S(1)} %get-tuple-element.22.refs_0_, f32[4,1024,128]{2,1,0:T(8,128)S(1)} %get-tuple-element.23.refs_1_, f32[4,128,128]{2,1,0:T(8,128)S(1)} %get-tuple-element.24.refs_2_, ...), custom_call_target="tpu_custom_call" | custom-call | flops 536870912 | bytes 4194304 | tf_op jit(solution)/shard_map/pallas_call | solution.py:311
  106.8 4.6 %collective-permute-start.24 = (bf16[128,2048]{1,0:T(8,128)(2,1)S(1)}, bf16[128,2048]{1,0:T(8,128)(2,1)S(1)}, u32[]{:S(2)}, u32[]{:S(2)}) collective-permute-start(bf16[128,2048]{1,0:T(8,128)(2,1)S(1)} %get-tuple-element.28), channel_id=1, source_target_pairs={{0,1},{1,0},{2,3},{3,2},{4,5},{5,4},{6,7},{7,6},{8,9},{9,8},{10,11... | collective-permute-start | bytes 1572872 | tf_op jit(solution)/shard_map/ppermute | solution.py:50
  113.0 1.3 %fusion = bf16[128,4096]{1,0:T(8,128)(2,1)} fusion(bf16[128,2048]{1,0:T(8,128)(2,1)S(1)} %collective-permute-done.24, bf16[128,2048]{1,0:T(8,128)(2,1)S(1)} %get-tuple-element.27, pred[128]{0:T(512)(128)(4,1)S(1)} %iota_compare_fusion, pred[]{:T(512)S(6)} %eq.6), kind=kLoop, calls=%fused_computation.1 | loop fusion | flops 5242880 | bytes 2097281 | tf_op jit(solution)/shard_map/jit(_where)/select_n | solution.py:408
  (55 shorter events, 10.6 us)
Async XLA Ops:
  0.0 5.9 %copy-start.4 = (s32[1,8]{1,0:T(1,128)S(1)}, s32[1,8]{1,0:T(1,128)}, u32[]{:S(2)}) copy-start(s32[1,8]{1,0:T(1,128)} %param.14) | copy-start | bytes 100
  0.0 7.7 %copy-start = (bf16[128,4096]{1,0:T(8,128)(2,1)S(1)}, bf16[128,4096]{1,0:T(8,128)(2,1)}, u32[]{:S(2)}) copy-start(bf16[128,4096]{1,0:T(8,128)(2,1)} %refs_0_.1) | copy-start | bytes 3145732
  1.4 6.8 %copy-start.1 = (bf16[128,512]{1,0:T(8,128)(2,1)S(1)}, bf16[128,512]{1,0:T(8,128)(2,1)}, u32[]{:S(2)}) copy-start(bf16[128,512]{1,0:T(8,128)(2,1)} %refs_2_.1) | copy-start | bytes 393220
  1.4 6.8 %copy-start.2 = (bf16[128,512]{1,0:T(8,128)(2,1)S(1)}, bf16[128,512]{1,0:T(8,128)(2,1)}, u32[]{:S(2)}) copy-start(bf16[128,512]{1,0:T(8,128)(2,1)} %refs_3_.1) | copy-start | bytes 393220
  1.4 25.3 %copy-start.3 = (s32[16]{0:T(128)S(1)}, s32[16]{0:T(128)}, u32[]{:S(2)}) copy-start(s32[16]{0:T(128)} %owner_ref.19) | copy-start | bytes 196
  1.4 23.3 %collective-permute-start.9 = (bf16[512,512]{1,0:T(8,128)(2,1)S(1)}, bf16[512,512]{1,0:T(8,128)(2,1)S(1)}, u32[]{:S(2)}, u32[]{:S(2)}) collective-permute-start(bf16[512,512]{1,0:T(8,128)(2,1)S(1)} %pad_maximum_fusion.refs_3_), channel_id=1, source_target_pairs={{4,8},{5,9},{6,10},{7,11},{8,4},{9,5},{10,6},{11,7},{20,24},{21,25... | collective-permute-start | bytes 1572872 | tf_op jit(solution)/shard_map/ppermute | solution.py:50
  4.8 23.3 %collective-permute-start.7 = (bf16[512,512]{1,0:T(8,128)(2,1)S(1)}, bf16[512,512]{1,0:T(8,128)(2,1)S(1)}, u32[]{:S(2)}, u32[]{:S(2)}) collective-permute-start(bf16[512,512]{1,0:T(8,128)(2,1)S(1)} %pad_maximum_fusion.refs_3_), channel_id=1, source_target_pairs={{0,4},{1,5},{2,6},{3,7},{4,0},{5,1},{6,2},{7,3},{8,12},{9,13},{10,... | collective-permute-start | bytes 1572872 | tf_op jit(solution)/shard_map/ppermute | solution.py:50
  4.9 15.6 %collective-permute-start.4 = (bf16[512,512]{1,0:T(8,128)(2,1)S(1)}, bf16[512,512]{1,0:T(8,128)(2,1)S(1)}, u32[]{:S(2)}, u32[]{:S(2)}) collective-permute-start(bf16[512,512]{1,0:T(8,128)(2,1)S(1)} %pad_maximum_fusion.1), channel_id=1, source_target_pairs={{0,1},{1,0},{2,3},{3,2},{4,5},{5,4},{6,7},{7,6},{8,9},{9,8},{10,11... | collective-permute-start | bytes 1572872 | tf_op jit(solution)/shard_map/ppermute | solution.py:50
  5.9 11.5 %collective-permute-start = (s32[1,8]{1,0:T(1,128)S(1)}, s32[1,8]{1,0:T(1,128)S(1)}, u32[]{:S(2)}, u32[]{:S(2)}) collective-permute-start(s32[1,8]{1,0:T(1,128)S(1)} %copy-done.4), channel_id=1, source_target_pairs={{0,4},{1,5},{2,6},{3,7},{4,0},{5,1},{6,2},{7,3},{8,12},{9,13},{10,... | collective-permute-start | bytes 104 | tf_op jit(solution)/shard_map/ppermute | solution.py:50
  7.7 30.5 %collective-permute-start.2 = (bf16[128,2048]{1,0:T(8,128)(2,1)S(1)}, bf16[128,2048]{1,0:T(8,128)(2,1)S(1)}, u32[]{:S(2)}, u32[]{:S(2)}) collective-permute-start(bf16[128,2048]{1,0:T(8,128)(2,1)S(1)} %slice_select_fusion), channel_id=1, source_target_pairs={{0,1},{1,0},{2,3},{3,2},{4,5},{5,4},{6,7},{7,6},{8,9},{9,8},{10,11... | collective-permute-start | bytes 1572872 | tf_op jit(solution)/shard_map/ppermute | solution.py:50
  17.4 2.8 %collective-permute-start.1 = (s32[2,8]{1,0:T(2,128)S(1)}, s32[2,8]{1,0:T(2,128)S(1)}, u32[]{:S(2)}, u32[]{:S(2)}) collective-permute-start(s32[2,8]{1,0:T(2,128)S(1)} %pad_add_fusion.1), channel_id=1, source_target_pairs={{0,1},{1,0},{2,3},{3,2},{4,5},{5,4},{6,7},{7,6},{8,9},{9,8},{10,11... | collective-permute-start | bytes 200 | tf_op jit(solution)/shard_map/ppermute | solution.py:50
  20.2 2.5 %collective-permute-start.5 = (s32[4,8]{1,0:T(4,128)S(1)}, s32[4,8]{1,0:T(4,128)S(1)}, u32[]{:S(2)}, u32[]{:S(2)}) collective-permute-start(s32[4,8]{1,0:T(4,128)S(1)} %pad_add_fusion), channel_id=1, source_target_pairs={{0,2},{1,3},{2,0},{3,1},{4,6},{5,7},{6,4},{7,5},{8,10},{9,11},{10,... | collective-permute-start | bytes 392 | tf_op jit(solution)/shard_map/ppermute | solution.py:50
  20.5 12.9 %collective-permute-start.8 = (bf16[512,512]{1,0:T(8,128)(2,1)S(1)}, bf16[512,512]{1,0:T(8,128)(2,1)S(1)}, u32[]{:S(2)}, u32[]{:S(2)}) collective-permute-start(bf16[512,512]{1,0:T(8,128)(2,1)S(1)} %collective-permute-done.4), channel_id=1, source_target_pairs={{0,4},{1,5},{2,6},{3,7},{4,0},{5,1},{6,2},{7,3},{8,12},{9,13},{10,... | collective-permute-start | bytes 1572872 | tf_op jit(solution)/shard_map/ppermute | solution.py:50
  22.7 17.1 %collective-permute-start.11 = (bf16[512,512]{1,0:T(8,128)(2,1)S(1)}, bf16[512,512]{1,0:T(8,128)(2,1)S(1)}, u32[]{:S(2)}, u32[]{:S(2)}) collective-permute-start(bf16[512,512]{1,0:T(8,128)(2,1)S(1)} %collective-permute-done.4), channel_id=1, source_target_pairs={{4,8},{5,9},{6,10},{7,11},{8,4},{9,5},{10,6},{11,7},{20,24},{21,25... | collective-permute-start | bytes 1572872 | tf_op jit(solution)/shard_map/ppermute | solution.py:50
  24.8 12.1 %collective-permute-start.3 = (bf16[128,512]{1,0:T(8,128)(2,1)S(1)}, bf16[128,512]{1,0:T(8,128)(2,1)S(1)}, u32[]{:S(2)}, u32[]{:S(2)}) collective-permute-start(bf16[128,512]{1,0:T(8,128)(2,1)S(1)} %pad_maximum_fusion.2), channel_id=1, source_target_pairs={{0,1},{1,0},{2,3},{3,2},{4,5},{5,4},{6,7},{7,6},{8,9},{9,8},{10,11... | collective-permute-start | bytes 393224 | tf_op jit(solution)/shard_map/ppermute | solution.py:50
  28.1 21.2 %collective-permute-start.17 = (bf16[512,512]{1,0:T(8,128)(2,1)S(1)}, bf16[512,512]{1,0:T(8,128)(2,1)S(1)}, u32[]{:S(2)}, u32[]{:S(2)}) collective-permute-start(bf16[512,512]{1,0:T(8,128)(2,1)S(1)} %collective-permute-done.7), channel_id=1, source_target_pairs={{4,8},{5,9},{6,10},{7,11},{8,4},{9,5},{10,6},{11,7},{20,24},{21,25... | collective-permute-start | bytes 1572872 | tf_op jit(solution)/shard_map/ppermute | solution.py:50
  33.3 25.7 %collective-permute-start.18 = (bf16[512,512]{1,0:T(8,128)(2,1)S(1)}, bf16[512,512]{1,0:T(8,128)(2,1)S(1)}, u32[]{:S(2)}, u32[]{:S(2)}) collective-permute-start(bf16[512,512]{1,0:T(8,128)(2,1)S(1)} %collective-permute-done.8), channel_id=1, source_target_pairs={{4,8},{5,9},{6,10},{7,11},{8,4},{9,5},{10,6},{11,7},{20,24},{21,25... | collective-permute-start | bytes 1572872 | tf_op jit(solution)/shard_map/ppermute | solution.py:50
  36.9 8.3 %collective-permute-start.13 = (bf16[2,128,512]{2,1,0:T(8,128)(2,1)S(1)}, bf16[2,128,512]{2,1,0:T(8,128)(2,1)S(1)}, u32[]{:S(2)}, u32[]{:S(2)}) collective-permute-start(bf16[2,128,512]{2,1,0:T(8,128)(2,1)S(1)} %get-tuple-element.16.refs_3_), channel_id=1, source_target_pairs={{4,0},{5,1},{6,2},{7,3},{8,12},{9,13},{10,14},{11,15},{20,16},{21,... | collective-permute-start | bytes 786440 | tf_op jit(solution)/shard_map/ppermute | solution.py:50
  38.3 9.8 %collective-permute-start.15 = (bf16[2,128,512]{2,1,0:T(8,128)(2,1)S(1)}, bf16[2,128,512]{2,1,0:T(8,128)(2,1)S(1)}, u32[]{:S(2)}, u32[]{:S(2)}) collective-permute-start(bf16[2,128,512]{2,1,0:T(8,128)(2,1)S(1)} %get-tuple-element.18), channel_id=1, source_target_pairs={{4,2},{5,3},{6,0},{7,1},{8,14},{9,15},{10,12},{11,13},{20,18},{21,... | collective-permute-start | bytes 786440 | tf_op jit(solution)/shard_map/ppermute | solution.py:50
  39.8 25.0 %collective-permute-start.6 = (bf16[4,128,512]{2,1,0:T(8,128)(2,1)S(1)}, bf16[4,128,512]{2,1,0:T(8,128)(2,1)S(1)}, u32[]{:S(2)}, u32[]{:S(2)}) collective-permute-start(bf16[4,128,512]{2,1,0:T(8,128)(2,1)S(1)} %shard_map.82.refs_3_), channel_id=1, source_target_pairs={{0,2},{1,3},{2,0},{3,1},{4,6},{5,7},{6,4},{7,5},{8,10},{9,11},{10,... | collective-permute-start | bytes 1572872 | tf_op jit(solution)/shard_map/ppermute | solution.py:50
  45.2 24.3 %collective-permute-start.12 = (bf16[4,128,512]{2,1,0:T(8,128)(2,1)S(1)}, bf16[4,128,512]{2,1,0:T(8,128)(2,1)S(1)}, u32[]{:S(2)}, u32[]{:S(2)}) collective-permute-start(bf16[4,128,512]{2,1,0:T(8,128)(2,1)S(1)} %shard_map.86.refs_3_), channel_id=1, source_target_pairs={{4,6},{5,7},{6,4},{7,5},{8,10},{9,11},{10,8},{11,9},{20,22},{21,23... | collective-permute-start | bytes 1572872 | tf_op jit(solution)/shard_map/ppermute | solution.py:50
  48.1 26.0 %collective-permute-start.10 = (bf16[4,128,512]{2,1,0:T(8,128)(2,1)S(1)}, bf16[4,128,512]{2,1,0:T(8,128)(2,1)S(1)}, u32[]{:S(2)}, u32[]{:S(2)}) collective-permute-start(bf16[4,128,512]{2,1,0:T(8,128)(2,1)S(1)} %shard_map.84.refs_3_), channel_id=1, source_target_pairs={{0,2},{1,3},{2,0},{3,1},{4,6},{5,7},{6,4},{7,5},{8,10},{9,11},{10,... | collective-permute-start | bytes 1572872 | tf_op jit(solution)/shard_map/ppermute | solution.py:50
  49.3 17.6 %collective-permute-start.14 = (bf16[2,128,512]{2,1,0:T(8,128)(2,1)S(1)}, bf16[2,128,512]{2,1,0:T(8,128)(2,1)S(1)}, u32[]{:S(2)}, u32[]{:S(2)}) collective-permute-start(bf16[2,128,512]{2,1,0:T(8,128)(2,1)S(1)} %get-tuple-element.17.refs_3_), channel_id=1, source_target_pairs={{4,0},{5,1},{6,2},{7,3},{8,12},{9,13},{10,14},{11,15},{20,16},{21,... | collective-permute-start | bytes 786440 | tf_op jit(solution)/shard_map/ppermute | solution.py:50
  59.0 9.2 %collective-permute-start.16 = (bf16[2,128,512]{2,1,0:T(8,128)(2,1)S(1)}, bf16[2,128,512]{2,1,0:T(8,128)(2,1)S(1)}, u32[]{:S(2)}, u32[]{:S(2)}) collective-permute-start(bf16[2,128,512]{2,1,0:T(8,128)(2,1)S(1)} %get-tuple-element.19), channel_id=1, source_target_pairs={{4,2},{5,3},{6,0},{7,1},{8,14},{9,15},{10,12},{11,13},{20,18},{21,... | collective-permute-start | bytes 786440 | tf_op jit(solution)/shard_map/ppermute | solution.py:50
  64.8 29.7 %collective-permute-start.19 = (bf16[4,128,512]{2,1,0:T(8,128)(2,1)S(1)}, bf16[4,128,512]{2,1,0:T(8,128)(2,1)S(1)}, u32[]{:S(2)}, u32[]{:S(2)}) collective-permute-start(bf16[4,128,512]{2,1,0:T(8,128)(2,1)S(1)} %shard_map.89.refs_18_.refs_10_), channel_id=1, source_target_pairs={{4,6},{5,7},{6,4},{7,5},{8,10},{9,11},{10,8},{11,9},{20,22},{21,23... | collective-permute-start | bytes 1572872 | tf_op jit(solution)/shard_map/ppermute | solution.py:50
  66.9 27.5 %collective-permute-start.20 = (bf16[2,128,512]{2,1,0:T(8,128)(2,1)S(1)}, bf16[2,128,512]{2,1,0:T(8,128)(2,1)S(1)}, u32[]{:S(2)}, u32[]{:S(2)}) collective-permute-start(bf16[2,128,512]{2,1,0:T(8,128)(2,1)S(1)} %get-tuple-element.20.refs_3_), channel_id=1, source_target_pairs={{4,0},{5,1},{6,2},{7,3},{8,12},{9,13},{10,14},{11,15},{20,16},{21,... | collective-permute-start | bytes 786440 | tf_op jit(solution)/shard_map/ppermute | solution.py:50
  68.3 26.2 %collective-permute-start.22 = (bf16[2,128,512]{2,1,0:T(8,128)(2,1)S(1)}, bf16[2,128,512]{2,1,0:T(8,128)(2,1)S(1)}, u32[]{:S(2)}, u32[]{:S(2)}) collective-permute-start(bf16[2,128,512]{2,1,0:T(8,128)(2,1)S(1)} %get-tuple-element.25), channel_id=1, source_target_pairs={{4,2},{5,3},{6,0},{7,1},{8,14},{9,15},{10,12},{11,13},{20,18},{21,... | collective-permute-start | bytes 786440 | tf_op jit(solution)/shard_map/ppermute | solution.py:50
  69.6 24.9 %collective-permute-start.21 = (bf16[2,128,512]{2,1,0:T(8,128)(2,1)S(1)}, bf16[2,128,512]{2,1,0:T(8,128)(2,1)S(1)}, u32[]{:S(2)}, u32[]{:S(2)}) collective-permute-start(bf16[2,128,512]{2,1,0:T(8,128)(2,1)S(1)} %get-tuple-element.21.refs_3_), channel_id=1, source_target_pairs={{4,0},{5,1},{6,2},{7,3},{8,12},{9,13},{10,14},{11,15},{20,16},{21,... | collective-permute-start | bytes 786440 | tf_op jit(solution)/shard_map/ppermute | solution.py:50
  74.0 20.5 %collective-permute-start.23 = (bf16[2,128,512]{2,1,0:T(8,128)(2,1)S(1)}, bf16[2,128,512]{2,1,0:T(8,128)(2,1)S(1)}, u32[]{:S(2)}, u32[]{:S(2)}) collective-permute-start(bf16[2,128,512]{2,1,0:T(8,128)(2,1)S(1)} %get-tuple-element.26), channel_id=1, source_target_pairs={{4,2},{5,3},{6,0},{7,1},{8,14},{9,15},{10,12},{11,13},{20,18},{21,... | collective-permute-start | bytes 786440 | tf_op jit(solution)/shard_map/ppermute | solution.py:50
  106.8 6.2 %collective-permute-start.24 = (bf16[128,2048]{1,0:T(8,128)(2,1)S(1)}, bf16[128,2048]{1,0:T(8,128)(2,1)S(1)}, u32[]{:S(2)}, u32[]{:S(2)}) collective-permute-start(bf16[128,2048]{1,0:T(8,128)(2,1)S(1)} %get-tuple-element.28), channel_id=1, source_target_pairs={{0,1},{1,0},{2,3},{3,2},{4,5},{5,4},{6,7},{7,6},{8,9},{9,8},{10,11... | collective-permute-start | bytes 1572872 | tf_op jit(solution)/shard_map/ppermute | solution.py:50
where the time goes:
time: 116 us; the launch traced here: 114 us
  starting transfers between devices  43.3 us (37%)
  Pallas kernels  42.5 us (37%)
  waiting for transfers between devices  24.4 us (21%)
  other arithmetic  2.9 us (2%)
    ppermute x25, starting transfers between devices, hop(): return lax.ppermute(x, 'rep', pairs)  43.3 us
    pallas_call x2, Pallas kernels, attend(): pl.pallas_call(functools.partial(attend_kernel, levels, first, final), ou...  30.9 us
    ppermute x25, waiting for transfers between devices, hop(): return lax.ppermute(x, 'rep', pairs)  24.4 us
    pallas_call x8, Pallas kernels, slots(): pl.pallas_call(functools.partial(slot_kernel, plane_of, dests, rels), out...  11.7 us
  transfers between devices with their start and end apart: 25, of which 8 were waited for; matrix products, arithmetic and copies ran while one was open for 0% of the time, Pallas kernels for 27%

commit v1 on v0

--- a/solution.py
+++ b/solution.py
@@ -19,6 +19,20 @@
 HALF_KV = HALF_HEADS * HEAD_SIZE
 HALF_Q = HALF_HEADS * GROUP * HEAD_SIZE
 SCALE2 = math.log2(math.e) / math.sqrt(HEAD_SIZE)
+
+GROUPS = (
+    (),
+    tuple(
+        (level, form, rel)
+        for level in range(2)
+        for form, rel in (("whole", 0), ("whole", 1), ("side", None))
+    )
+    + ((2, "whole", 0), (2, "whole", 1), (2, "side", None))
+    + ((2, "end", 0), (2, "end", 1), (2, "end_side", 0), (2, "end_side", 1)),
+    ((3, "whole", 0), (3, "side", 0), (3, "end", 0), (3, "end_side", 0)),
+    ((3, "whole", 1), (3, "side", 1), (3, "end", 1), (3, "end_side", 1)),
+)
+ROOMS = (0, 8, 2, 2)
 
 
 SMEM = pl.BlockSpec(memory_space=pltpu.SMEM)
@@ -105,7 +119,7 @@
     s_ref[:, :width] = lax.dot_general(
         query, held_of(pieces, 0), (((1,), (1,)), ((), ())), preferred_element_type=jnp.float32
     )
-    scales, tops, totals = [], [], []
+    scales, totals = [], []
     for h in range(GROUP):
         rows = slice(h * BLK, (h + 1) * BLK)
         parts = []
@@ -113,13 +127,13 @@
             part = s_ref[rows, j * BLK : (j + 1) * BLK]
             if prompt and j == 0:
                 part = jnp.where(col <= row, part, -jnp.inf)
-            elif j == pieces - 1:
+            elif j == pieces - 1 and odd is not None:
                 part = jnp.where(odd, -jnp.inf, part)
             parts.append(part)
         top = functools.reduce(jnp.maximum, parts)
-        top = jnp.max(top, axis=1, keepdims=True)
+        top = jnp.broadcast_to(jnp.max(top, axis=1, keepdims=True), (BLK, BLK))
         if state_in is not None:
-            before = state_in[1][:, h : h + 1]
+            before = state_in[1][rows]
             top = jnp.maximum(top, before)
             scale = jnp.exp2((before - top) * SCALE2)
             scales.append(scale)
@@ -128,18 +142,20 @@
             weight = jnp.exp2((part - top) * SCALE2)
             total = weight if total is None else total + weight
             p_ref[rows, j * BLK : (j + 1) * BLK] = weight.astype(jnp.bfloat16)
-        total = jnp.sum(total, axis=1, keepdims=True)
+        total = jnp.broadcast_to(jnp.sum(total, axis=1, keepdims=True), (BLK, BLK))
         if state_in is not None:
-            total = total + scale * state_in[1][:, GROUP + h : GROUP + h + 1]
-        tops.append(top)
-        totals.append(total)
+            total = total + scale * state_in[2][rows]
+        if out is None:
+            state_out[1][rows] = top
+            state_out[2][rows] = total
+        else:
+            totals.append(total)
     mixed = lax.dot_general(
         p_ref[:, :width],
         held_of(pieces, 1),
         (((1,), (0,)), ((), ())),
         preferred_element_type=jnp.float32,
     )
-    stats = jnp.zeros((BLK, BLK), jnp.float32)
     for h in range(GROUP):
         rows = slice(h * BLK, (h + 1) * BLK)
         value = mixed[rows]
@@ -149,71 +165,79 @@
             out(h, (value * (1.0 / totals[h])).astype(jnp.bfloat16))
         else:
             state_out[0][rows] = value
-            stats = jnp.where(col == h, tops[h], stats)
-            stats = jnp.where(col == GROUP + h, totals[h], stats)
-    if out is None:
-        state_out[1][...] = stats
-
-
-def attend_kernel(levels, first, final, owner_ref, list_ref, *refs):
+
+
+def attend_kernel(group, owner_ref, list_ref, *refs):
+    first, final = group == 0, group == len(GROUPS) - 1
     refs = list(refs)
     if first:
         q_ref, pair_q_ref, kp_ref, vp_ref, pair_kv_ref = refs[:5]
         refs = refs[5:]
     else:
-        stacked_ref, acc_ref, stats_ref = refs[:3]
-        refs = refs[3:]
-    table = source_table(levels)
+        stacked_ref, acc_ref, top_ref, total_ref, plan_ref = refs[:5]
+        refs = refs[5:]
+    table = GROUPS[group]
     sources, refs = refs[: len(table)], refs[len(table) + 1 :]
     if first:
-        stacked_ref = refs.pop(0)
+        stacked_ref, plan_ref = refs[:2]
+        refs = refs[2:]
     if final:
         out_ref = refs.pop(0)
     else:
-        acc_out, stats_out = refs.pop(0), refs.pop(0)
-    held, s_ref, p_ref, count_ref, sems = refs
-    room = min(4 * len(levels), LIST)
+        acc_out, top_out, total_out = refs[:3]
+        refs = refs[3:]
+    held, s_ref, p_ref, sems = refs
+    room = ROOMS[group]
     base = 1 if first else 0
     z, y, c = place()
-    near = z ^ 1
-    mid = jnp.logical_or(z == 1, z == 2)
-    inner = jnp.where(mid, 3 - z, 3 - near)
-    for d in range(2):
-
-        def fetch(j, count, d=d):
-            block = list_ref[d, j]
-            owner = owner_ref[block // SPAN_BLK]
-            oz, oy, oc = owner // 4, (owner // 2) % 2, owner % 2
-            rel = (oc != c).astype(jnp.int32)
-            level = jnp.where(oz == z, 0, jnp.where(oz == near, 1, jnp.where(oz == inner, 2, 3)))
-            own_column = oy == y
-            whole = jnp.logical_and(own_column, jnp.logical_or(level < 2, mid))
-            spot_whole = block % SPAN_BLK
-            listed = functools.reduce(jnp.logical_or, [level == one for one in levels])
-            for (at_level, form, at_rel), source in zip(table, sources):
-                if form == "whole":
-                    match = jnp.logical_and(whole, rel == at_rel)
-                    spot = spot_whole
-                elif form == "side":
-                    match = jnp.logical_and(~own_column, jnp.logical_or(level < 2, mid))
-                    spot = d * 2 + rel
-                else:
-                    match = jnp.logical_and(
-                        ~mid, own_column if form == "end" else ~own_column
-                    )
-                    match = jnp.logical_and(match, rel == at_rel)
-                    spot = d
-                match = jnp.logical_and(match, level == at_level)
-
-                @pl.when(match)
-                def _(source=source, spot=spot):
+    if first:
+        near = z ^ 1
+        mid = jnp.logical_or(z == 1, z == 2)
+        inner = jnp.where(mid, 3 - z, 3 - near)
+        for d in range(2):
+            for at in range(len(GROUPS)):
+                plan_ref[at, d, 0] = jnp.int32(0)
+
+            def place_block(j, carry, d=d):
+                block = list_ref[d, j]
+                owner = owner_ref[block // SPAN_BLK]
+                oz, oy, oc = owner // 4, (owner // 2) % 2, owner % 2
+                rel = (oc != c).astype(jnp.int32)
+                level = jnp.where(
+                    oz == z, 0, jnp.where(oz == near, 1, jnp.where(oz == inner, 2, 3))
+                )
+                own_column = oy == y
+                direct = jnp.logical_or(level < 2, mid)
+                whole = jnp.logical_and(own_column, direct)
+                slot = jnp.where(jnp.logical_and(direct, level < 3), d * 2 + rel, d)
+                spot = jnp.where(whole, block % SPAN_BLK, slot)
+                side = jnp.where(own_column, 0, 1)
+                form = jnp.where(whole, rel, jnp.where(direct, 2, 3 + side * 2 + rel))
+                last_form = jnp.where(whole, 0, jnp.where(direct, 1, 2 + side))
+                to = jnp.where(level == 3, 2 + rel, 1)
+                index = jnp.where(level == 3, last_form, form + level * 3)
+                count = plan_ref[to, d, 0]
+                plan_ref[to, d, 1 + count] = index * 8 + spot
+                plan_ref[to, d, 0] = count + 1
+                return carry
+
+            lax.fori_loop(0, LIST, place_block, 0)
+
+    for d in range(2 if room else 0):
+
+        def fetch(j, carry, d=d):
+            code = plan_ref[group, d, 1 + j]
+            for at, source in enumerate(sources):
+
+                @pl.when(code // 8 == at)
+                def _(source=source):
                     pltpu.make_async_copy(
-                        source.at[spot], held.at[d, base + count], sems.at[d, count]
+                        source.at[code % 8], held.at[d, base + j], sems.at[d, j]
                     ).start()
 
-            return count + listed.astype(jnp.int32)
-
-        count_ref[d] = lax.fori_loop(0, LIST, fetch, jnp.int32(0))
+            return carry
+
+        lax.fori_loop(0, plan_ref[group, d, 0], fetch, 0)
 
     if first:
         for g in range(HALF_HEADS):
@@ -230,19 +254,26 @@
 
     def part(i, carry):
         d, g = i // HALF_HEADS, i % HALF_HEADS
-        count = count_ref[d]
-
-        @pl.when(g == 0)
-        def _():
-            def arrive(j, carry):
-                pltpu.make_async_copy(sources[0].at[0], held.at[d, base + j], sems.at[d, j]).wait()
-                return carry
-
-            lax.fori_loop(0, count, arrive, 0)
-
-            @pl.when(count % 2 == 1)
+        count = plan_ref[group, d, 0]
+        pairs = room > 2
+
+        if room:
+
+            @pl.when(g == 0)
             def _():
-                held[d, base + count] = jnp.zeros((BLK, 2 * HALF_KV), jnp.bfloat16)
+                def arrive(j, carry):
+                    pltpu.make_async_copy(
+                        sources[0].at[0], held.at[d, base + j], sems.at[d, j]
+                    ).wait()
+                    return carry
+
+                lax.fori_loop(0, count, arrive, 0)
+
+                if pairs:
+
+                    @pl.when(count % 2 == 1)
+                    def _():
+                        held[d, base + count] = jnp.zeros((BLK, 2 * HALF_KV), jnp.bfloat16)
 
         def held_of(pieces, which):
             at = pl.multiple_of(which * HALF_KV + g * HEAD_SIZE, HEAD_SIZE)
@@ -255,30 +286,30 @@
                 at = pl.multiple_of((g * GROUP + h) * HEAD_SIZE, HEAD_SIZE)
                 out_ref[d, :, pl.ds(at, HEAD_SIZE)] = value
 
-        for even in range(0, room + 1, 2):
-
-            @pl.when((count + 1) // 2 * 2 == even)
+        for even in range(0, room + 1, 2 if pairs else 1):
+
+            @pl.when(((count + 1) // 2 * 2 if pairs else count if room else 0) == even)
             def _(even=even):
                 if even == 0 and not first:
-                    if final:
-                        for h in range(GROUP):
-                            value = acc_ref[i, h * BLK : (h + 1) * BLK, :]
-                            total = stats_ref[i, :, GROUP + h : GROUP + h + 1]
-                            out(h, (value * (1.0 / total)).astype(jnp.bfloat16))
-                    else:
+                    if not final:
                         acc_out[i] = acc_ref[i]
-                        stats_out[i] = stats_ref[i]
+                        top_out[i] = top_ref[i]
+                        total_out[i] = total_ref[i]
+                        return
+                    for h in range(GROUP):
+                        rows = slice(h * BLK, (h + 1) * BLK)
+                        out(h, (acc_ref[i, rows] * (1.0 / total_ref[i, rows])).astype(jnp.bfloat16))
                     return
                 softmax_part(
                     even,
-                    count % 2 == 1,
+                    count % 2 == 1 if pairs else None,
                     first,
                     held_of,
                     stacked_ref[i],
                     s_ref,
                     p_ref,
-                    None if first else (acc_ref.at[i], stats_ref.at[i]),
-                    None if final else (acc_out.at[i], stats_out.at[i]),
+                    None if first else (acc_ref.at[i], top_ref.at[i], total_ref.at[i]),
+                    None if final else (acc_out.at[i], top_out.at[i], total_out.at[i]),
                     out,
                 )
 
@@ -287,50 +318,39 @@
     lax.fori_loop(0, 2 * HALF_HEADS, part, 0)
 
 
-def source_table(levels):
-    table = []
-    for level in levels:
-        table += [(level, "whole", 0), (level, "whole", 1), (level, "side", None)]
-        if level > 1:
-            table += [(level, form, rel) for form in ("end", "end_side") for rel in range(2)]
-    return table
-
-
-def attend(levels, first, final, owner, lists, operands, sources, after):
+def attend(group, owner, lists, operands, sources, after):
+    first, final = group == 0, group == len(GROUPS) - 1
     parts = 2 * HALF_HEADS
-    room = min(4 * len(levels), LIST)
+    room = ROOMS[group]
     pieces = room + (1 if first else 0)
     rows = GROUP * BLK
     stacked = jax.ShapeDtypeStruct((parts, rows, HEAD_SIZE), jnp.bfloat16)
-    acc = jax.ShapeDtypeStruct((parts, rows, HEAD_SIZE), jnp.float32)
-    stats = jax.ShapeDtypeStruct((parts, BLK, BLK), jnp.float32)
-    outs = [stacked] if first else []
-    outs += [jax.ShapeDtypeStruct((2, BLK, HALF_Q), jnp.bfloat16)] if final else [acc, stats]
-    used = sources_of(levels, sources)
+    state = jax.ShapeDtypeStruct((parts, rows, HEAD_SIZE), jnp.float32)
+    plan = jax.ShapeDtypeStruct((len(GROUPS), 2, 1 + LIST), jnp.int32)
+    outs = [stacked, plan] if first else []
+    outs += [jax.ShapeDtypeStruct((2, BLK, HALF_Q), jnp.bfloat16)] if final else [state] * 3
+    used = [sources[key].reshape(-1, BLK, 2 * HALF_KV) for key in GROUPS[group]]
     keys = (pieces + 1) // 2 * BLK
     return pl.pallas_call(
-        functools.partial(attend_kernel, levels, first, final),
+        functools.partial(attend_kernel, group),
         out_shape=outs,
-        in_specs=[SMEM] * 2 + [VMEM] * len(operands) + [ANY] * (len(used) + 1),
-        out_specs=[VMEM] * len(outs),
+        in_specs=[SMEM] * 2
+        + ([VMEM] * 5 if first else [VMEM] * 4 + [SMEM])
+        + [ANY] * (len(used) + 1),
+        out_specs=[SMEM if out is plan else VMEM for out in outs],
         scratch_shapes=[
-            pltpu.VMEM((2, room + 1, BLK, 2 * HALF_KV), jnp.bfloat16),
+            pltpu.VMEM((2, pieces, BLK, 2 * HALF_KV), jnp.bfloat16),
             pltpu.VMEM((rows, pieces * BLK), jnp.float32),
             pltpu.VMEM((rows, pieces * BLK), jnp.bfloat16),
-            pltpu.SMEM((2,), jnp.int32),
-            pltpu.SemaphoreType.DMA((2, room)),
+            pltpu.SemaphoreType.DMA((2, max(room, 1))),
         ],
         cost_estimate=pl.CostEstimate(
             flops=4 * QUERY_HEADS * BLK * keys * HEAD_SIZE,
             bytes_accessed=4 << 20,
             transcendentals=QUERY_HEADS * BLK * keys,
         ),
-        compiler_params=pltpu.CompilerParams(vmem_limit_bytes=30 << 20),
+        compiler_params=pltpu.CompilerParams(vmem_limit_bytes=28 << 20),
     )(owner, lists, *operands, *used, after)
-
-
-def sources_of(levels, sources):
-    return [sources[key].reshape(-1, BLK, 2 * HALF_KV) for key in source_table(levels)]
 
 
 def line_device(
@@ -382,10 +402,13 @@
         return side
 
     def send_end(level, rel, after):
-        end, end_side = slots(planes[level], span_owner, near_lists, spans[level], (rel,), after)
-        sources[level, "end", rel] = hop(end, END)
-        sources[level, "end_side", rel] = hop(end_side, END_SIDE)
-        return end
+        dests = near_lists + ([side_lists] if level == 3 else [])
+        outs = slots(planes[level], span_owner, dests, spans[level], (rel,), after)
+        sources[level, "end", rel] = hop(outs[0], END)
+        sources[level, "end_side", rel] = hop(outs[1], END_SIDE)
+        if level == 3:
+            sources[level, "side", rel] = hop(outs[2], MID_SIDE)
+        return outs[0]
 
     last = send_side(0, own[0])
     last = send_end(2, 0, last)
@@ -393,11 +416,13 @@
     last = send_end(2, 1, last)
     last = send_side(2, last)
     last = send_end(3, 0, last)
-    last = send_end(3, 1, last)
-    last = send_side(3, last)
     operands = [queries, pair_q, prompt_keys, prompt_value_rows, pair_kv]
-    operands = attend((0, 1, 2), True, False, span_owner, lists, operands, sources, last)
-    (halves,) = attend((3,), False, True, span_owner, lists, operands, sources, last)
+    stacked, plan, *state = attend(0, span_owner, lists, operands, sources, last)
+    last = send_end(3, 1, state[0])
+    for group in (1, 2):
+        operands = [stacked, *state, plan]
+        state = attend(group, span_owner, lists, operands, sources, last)
+    (halves,) = attend(3, span_owner, lists, [stacked, *state, plan], sources, last)
     mine, theirs = halves[0], hop(halves[1], CORE)
     joined = jnp.where(
         first,

time: 116 us -> 109 us (0.940)
  Pallas kernels: 42.5 us -> 33.2 us
  starting transfers between devices: 43.3 us -> 44.8 us
    pallas_call x2 -> x4, Pallas kernels: 30.9 us -> 22 us  [attend(): pl.pallas_call(functools.partial(attend_kernel, group), out_shape=outs, i...]
    ppermute x25 -> x26, starting transfers between devices: 43.3 us -> 44.8 us  [hop(): return lax.ppermute(x, 'rep', pairs)]
    ppermute x25 -> x26, waiting for transfers between devices: 24.4 us -> 25.2 us  [hop(): return lax.ppermute(x, 'rep', pairs)]
    pallas_call x8 -> x7, Pallas kernels: 11.7 us -> 11.2 us  [slots(): pl.pallas_call(functools.partial(slot_kernel, plane_of, dests, rels), out...]
  transfers between devices with their start and end apart: 25 -> 26, of which waited for: 8 -> 7; matrix products, arithmetic and copies ran while one was open for 0% -> 0% of each run, Pallas kernels for 27% -> 28%
where the time goes in v1:
time: 109 us; the launch traced here: 107 us
  starting transfers between devices  44.8 us (41%)
  Pallas kernels  33.2 us (30%)
  waiting for transfers between devices  25.2 us (23%)
  other arithmetic  2.93 us (3%)
  between operations  1.1 us (1%)
    ppermute x26, starting transfers between devices, hop(): return lax.ppermute(x, 'rep', pairs)  44.8 us
    ppermute x26, waiting for transfers between devices, hop(): return lax.ppermute(x, 'rep', pairs)  25.2 us
    pallas_call x4, Pallas kernels, attend(): pl.pallas_call(functools.partial(attend_kernel, group), out_shape=outs, i...  22 us
    pallas_call x7, Pallas kernels, slots(): pl.pallas_call(functools.partial(slot_kernel, plane_of, dests, rels), out...  11.2 us
  transfers between devices with their start and end apart: 26, of which 7 were waited for; matrix products, arithmetic and copies ran while one was open for 0% of the time, Pallas kernels for 28%

profile of v1, /device:TPU:15, one launch (start us, length us, event | category | flops | bytes accessed | tf_op | source)
XLA Modules:
  0.0 107.3 jit_solution(15126886616123785418)
XLA Ops:
  0.0 1.4 %broadcast_select_fusion = (bf16[512,256]{1,0:T(8,128)(2,1)S(1)}, bf16[512,256]{1,0:T(8,128)(2,1)S(1)}, bf16[512,256]{1,0:T(8,128)(2,1)S(1)}, bf16[512,256]{1,0:T(8,128)(2,1)S(1)}) fusion(pred[]{:T(512)S(6)} %eq.7, bf16[512,512]{1,0:T(8,128)(2,1)} %param.12, pred[]{:T(512)S(6)} %eq.6, bf16[512,512]{1,0:T(8,128)(2,1)} %param.11), kind=kLoop, calls=%fused_computation.7 | loop fusion | flops 524288 | bytes 2097154 | tf_op jit(solution)/shard_map/jit(_where)/select_n | solution.py:370
  1.4 3.2 %collective-permute-start.7 = (bf16[512,512]{1,0:T(8,128)(2,1)S(1)}, bf16[512,512]{1,0:T(8,128)(2,1)S(1)}, u32[]{:S(2)}, u32[]{:S(2)}) collective-permute-start(bf16[512,512]{1,0:T(8,128)(2,1)S(1)} %pad_maximum_fusion.refs_3_), channel_id=1, source_target_pairs={{4,8},{5,9},{6,10},{7,11},{8,4},{9,5},{10,6},{11,7},{20,24},{21,25... | collective-permute-start | bytes 1572872 | tf_op jit(solution)/shard_map/ppermute | solution.py:64
  5.8 1.7 %collective-permute-start = (s32[1,8]{1,0:T(1,128)S(1)}, s32[1,8]{1,0:T(1,128)S(1)}, u32[]{:S(2)}, u32[]{:S(2)}) collective-permute-start(s32[1,8]{1,0:T(1,128)S(1)} %copy-done.4), channel_id=1, source_target_pairs={{0,4},{1,5},{2,6},{3,7},{4,0},{5,1},{6,2},{7,3},{8,12},{9,13},{10,... | collective-permute-start | bytes 104 | tf_op jit(solution)/shard_map/ppermute | solution.py:64
  8.0 9.2 %collective-permute-done = s32[1,8]{1,0:T(1,128)S(1)} collective-permute-done((s32[1,8]{1,0:T(1,128)S(1)}, s32[1,8]{1,0:T(1,128)S(1)}, u32[]{:S(2)}, u32[]{:S(2)}) %collective-permute-start) | collective-permute-done | bytes 64 | tf_op jit(solution)/shard_map/ppermute | solution.py:64
  17.3 2.0 %collective-permute-start.1 = (s32[2,8]{1,0:T(2,128)S(1)}, s32[2,8]{1,0:T(2,128)S(1)}, u32[]{:S(2)}, u32[]{:S(2)}) collective-permute-start(s32[2,8]{1,0:T(2,128)S(1)} %pad_add_fusion.1), channel_id=1, source_target_pairs={{0,1},{1,0},{2,3},{3,2},{4,5},{5,4},{6,7},{7,6},{8,9},{9,8},{10,11... | collective-permute-start | bytes 200 | tf_op jit(solution)/shard_map/ppermute | solution.py:64
  20.3 2.2 %collective-permute-done.4 = s32[4,8]{1,0:T(4,128)S(1)} collective-permute-done((s32[4,8]{1,0:T(4,128)S(1)}, s32[4,8]{1,0:T(4,128)S(1)}, u32[]{:S(2)}, u32[]{:S(2)}) %collective-permute-start.4) | collective-permute-done | bytes 160 | tf_op jit(solution)/shard_map/ppermute | solution.py:64
  22.6 1.5 %collective-permute-start.2 = (bf16[128,2048]{1,0:T(8,128)(2,1)S(1)}, bf16[128,2048]{1,0:T(8,128)(2,1)S(1)}, u32[]{:S(2)}, u32[]{:S(2)}) collective-permute-start(bf16[128,2048]{1,0:T(8,128)(2,1)S(1)} %slice_select_fusion), channel_id=1, source_target_pairs={{0,1},{1,0},{2,3},{3,2},{4,5},{5,4},{6,7},{7,6},{8,9},{9,8},{10,11... | collective-permute-start | bytes 1572872 | tf_op jit(solution)/shard_map/ppermute | solution.py:64
  24.1 2.1 %collective-permute-start.9 = (bf16[512,512]{1,0:T(8,128)(2,1)S(1)}, bf16[512,512]{1,0:T(8,128)(2,1)S(1)}, u32[]{:S(2)}, u32[]{:S(2)}) collective-permute-start(bf16[512,512]{1,0:T(8,128)(2,1)S(1)} %collective-permute-done.8), channel_id=1, source_target_pairs={{4,8},{5,9},{6,10},{7,11},{8,4},{9,5},{10,6},{11,7},{20,24},{21,25... | collective-permute-start | bytes 1572872 | tf_op jit(solution)/shard_map/ppermute | solution.py:64
  26.2 3.2 %collective-permute-start.6 = (bf16[512,512]{1,0:T(8,128)(2,1)S(1)}, bf16[512,512]{1,0:T(8,128)(2,1)S(1)}, u32[]{:S(2)}, u32[]{:S(2)}) collective-permute-start(bf16[512,512]{1,0:T(8,128)(2,1)S(1)} %collective-permute-done.5), channel_id=1, source_target_pairs={{4,8},{5,9},{6,10},{7,11},{8,4},{9,5},{10,6},{11,7},{20,24},{21,25... | collective-permute-start | bytes 1572872 | tf_op jit(solution)/shard_map/ppermute | solution.py:64
  29.4 1.4 %shard_map.82.refs_3_ = bf16[4,128,512]{2,1,0:T(8,128)(2,1)S(1)} custom-call(s32[16]{0:T(128)S(1)} %copy-done.3, s32[2,8]{1,0:T(2,128)S(1)} %pad_add_fusion.5.refs_0_.refs_2_, bf16[4,128,512]{2,1,0:T(8,128)(2,1)S(1)} %bitcast.14, bf16[4,128,512]{2,1,0:T(8,128)(2,1)S(1)} %bitcast.26, bf16[512,512]{1,0:T(8,128)(2,1)S(1)} %pad_maximum_fusion.refs_3_), custom_call_target="tpu_custom_call" | custom-call | bytes 1048576 | tf_op jit(solution)/shard_map/pallas_call | solution.py:103
  31.1 1.5 %shard_map.83 = (bf16[2,128,512]{2,1,0:T(8,128)(2,1)S(1)}, bf16[2,128,512]{2,1,0:T(8,128)(2,1)S(1)}) custom-call(s32[16]{0:T(128)S(1)} %copy-done.3, s32[2,8]{1,0:T(2,128)S(1)} %pad_add_fusion.3.refs_0_, s32[2,8]{1,0:T(2,128)S(1)} %pad_add_fusion.4.refs_1_, bf16[4,128,512]{2,1,0:T(8,128)(2,1)S(1)} %bitcast.16, bf16[4,128,512]{2,1,0:T(8,128)(2,1)S(1)} %shard_map.82.refs_3_), custom_call_target="tpu_custom_call" | custom-call | bytes 1048576 | tf_op jit(solution)/shard_map/pallas_call | solution.py:103
  32.7 1.3 %collective-permute-start.14 = (bf16[2,128,512]{2,1,0:T(8,128)(2,1)S(1)}, bf16[2,128,512]{2,1,0:T(8,128)(2,1)S(1)}, u32[]{:S(2)}, u32[]{:S(2)}) collective-permute-start(bf16[2,128,512]{2,1,0:T(8,128)(2,1)S(1)} %get-tuple-element.26.refs_3_), channel_id=1, source_target_pairs={{4,0},{5,1},{6,2},{7,3},{8,12},{9,13},{10,14},{11,15},{20,16},{21,... | collective-permute-start | bytes 786440 | tf_op jit(solution)/shard_map/ppermute | solution.py:64
  34.0 3.5 %collective-permute-done.10 = bf16[512,512]{1,0:T(8,128)(2,1)S(1)} collective-permute-done((bf16[512,512]{1,0:T(8,128)(2,1)S(1)}, bf16[512,512]{1,0:T(8,128)(2,1)S(1)}, u32[]{:S(2)}, u32[]{:S(2)}) %collective-permute-start.10) | collective-permute-done | bytes 524320 | tf_op jit(solution)/shard_map/ppermute | solution.py:64
  37.5 1.9 %collective-permute-start.16 = (bf16[2,128,512]{2,1,0:T(8,128)(2,1)S(1)}, bf16[2,128,512]{2,1,0:T(8,128)(2,1)S(1)}, u32[]{:S(2)}, u32[]{:S(2)}) collective-permute-start(bf16[2,128,512]{2,1,0:T(8,128)(2,1)S(1)} %get-tuple-element.34), channel_id=1, source_target_pairs={{4,2},{5,3},{6,0},{7,1},{8,14},{9,15},{10,12},{11,13},{20,18},{21,... | collective-permute-start | bytes 786440 | tf_op jit(solution)/shard_map/ppermute | solution.py:64
  39.4 2.1 %collective-permute-start.18 = (bf16[512,512]{1,0:T(8,128)(2,1)S(1)}, bf16[512,512]{1,0:T(8,128)(2,1)S(1)}, u32[]{:S(2)}, u32[]{:S(2)}) collective-permute-start(bf16[512,512]{1,0:T(8,128)(2,1)S(1)} %collective-permute-done.10), channel_id=1, source_target_pairs={{4,8},{5,9},{6,10},{7,11},{8,4},{9,5},{10,6},{11,7},{20,24},{21,25... | collective-permute-start | bytes 1572872 | tf_op jit(solution)/shard_map/ppermute | solution.py:64
  41.5 1.4 %shard_map.84.refs_3_ = bf16[4,128,512]{2,1,0:T(8,128)(2,1)S(1)} custom-call(s32[16]{0:T(128)S(1)} %copy-done.3, s32[2,8]{1,0:T(2,128)S(1)} %pad_add_fusion.5.refs_0_.refs_2_, bf16[4,128,512]{2,1,0:T(8,128)(2,1)S(1)} %bitcast.24, bf16[4,128,512]{2,1,0:T(8,128)(2,1)S(1)} %bitcast.28, bf16[2,128,512]{2,1,0:T(8,128)(2,1)S(1)} %get-tuple-element.26.refs_3_), custom_call_target="tpu_custom_call" | custom-call | bytes 1048576 | tf_op jit(solution)/shard_map/pallas_call | solution.py:103
  42.9 1.5 %shard_map.85 = (bf16[2,128,512]{2,1,0:T(8,128)(2,1)S(1)}, bf16[2,128,512]{2,1,0:T(8,128)(2,1)S(1)}) custom-call(s32[16]{0:T(128)S(1)} %copy-done.3, s32[2,8]{1,0:T(2,128)S(1)} %pad_add_fusion.3.refs_0_, s32[2,8]{1,0:T(2,128)S(1)} %pad_add_fusion.4.refs_1_, bf16[4,128,512]{2,1,0:T(8,128)(2,1)S(1)} %bitcast.19, bf16[4,128,512]{2,1,0:T(8,128)(2,1)S(1)} %shard_map.84.refs_3_), custom_call_target="tpu_custom_call" | custom-call | bytes 1048576 | tf_op jit(solution)/shard_map/pallas_call | solution.py:103
  45.8 1.4 %shard_map.86.refs_4_ = bf16[4,128,512]{2,1,0:T(8,128)(2,1)S(1)} custom-call(s32[16]{0:T(128)S(1)} %copy-done.3, s32[2,8]{1,0:T(2,128)S(1)} %pad_add_fusion.5.refs_0_.refs_2_, bf16[4,128,512]{2,1,0:T(8,128)(2,1)S(1)} %bitcast.17, bf16[4,128,512]{2,1,0:T(8,128)(2,1)S(1)} %bitcast.20, bf16[2,128,512]{2,1,0:T(8,128)(2,1)S(1)} %get-tuple-element.27.refs_3_), custom_call_target="tpu_custom_call" | custom-call | bytes 1048576 | tf_op jit(solution)/shard_map/pallas_call | solution.py:103
  47.2 3.1 %collective-permute-start.13 = (bf16[4,128,512]{2,1,0:T(8,128)(2,1)S(1)}, bf16[4,128,512]{2,1,0:T(8,128)(2,1)S(1)}, u32[]{:S(2)}, u32[]{:S(2)}) collective-permute-start(bf16[4,128,512]{2,1,0:T(8,128)(2,1)S(1)} %shard_map.86.refs_4_), channel_id=1, source_target_pairs={{4,6},{5,7},{6,4},{7,5},{8,10},{9,11},{10,8},{11,9},{20,22},{21,23... | collective-permute-start | bytes 1572872 | tf_op jit(solution)/shard_map/ppermute | solution.py:64
  50.6 1.7 %collective-permute-start.17 = (bf16[2,128,512]{2,1,0:T(8,128)(2,1)S(1)}, bf16[2,128,512]{2,1,0:T(8,128)(2,1)S(1)}, u32[]{:S(2)}, u32[]{:S(2)}) collective-permute-start(bf16[2,128,512]{2,1,0:T(8,128)(2,1)S(1)} %get-tuple-element.35), channel_id=1, source_target_pairs={{4,2},{5,3},{6,0},{7,1},{8,14},{9,15},{10,12},{11,13},{20,18},{21,... | collective-permute-start | bytes 786440 | tf_op jit(solution)/shard_map/ppermute | solution.py:64
  52.4 2.0 %shard_map.87 = (bf16[2,128,512]{2,1,0:T(8,128)(2,1)S(1)}, bf16[2,128,512]{2,1,0:T(8,128)(2,1)S(1)}, bf16[2,128,512]{2,1,0:T(8,128)(2,1)S(1)}) custom-call(s32[16]{0:T(128)S(1)} %copy-done.3, s32[2,8]{1,0:T(2,128)S(1)} %pad_add_fusion.3.refs_0_, s32[2,8]{1,0:T(2,128)S(1)} %pad_add_fusion.4.refs_1_, s32[2,8]{1,0:T(2,128)S(1)} %pad_add_fusion.5.refs_0_.refs_2_, ...), custom_call_target="tpu_custom_call" | custom-call | bytes 1572864 | tf_op jit(solution)/shard_map/pallas_call | solution.py:103
  54.4 3.3 %collective-permute-start.19 = (bf16[2,128,512]{2,1,0:T(8,128)(2,1)S(1)}, bf16[2,128,512]{2,1,0:T(8,128)(2,1)S(1)}, u32[]{:S(2)}, u32[]{:S(2)}) collective-permute-start(bf16[2,128,512]{2,1,0:T(8,128)(2,1)S(1)} %get-tuple-element.40), channel_id=1, source_target_pairs={{4,6},{5,7},{6,4},{7,5},{8,10},{9,11},{10,8},{11,9},{20,22},{21,23... | collective-permute-start | bytes 786440 | tf_op jit(solution)/shard_map/ppermute | solution.py:64
  57.8 4.0 %collective-permute-start.20 = (bf16[2,128,512]{2,1,0:T(8,128)(2,1)S(1)}, bf16[2,128,512]{2,1,0:T(8,128)(2,1)S(1)}, u32[]{:S(2)}, u32[]{:S(2)}) collective-permute-start(bf16[2,128,512]{2,1,0:T(8,128)(2,1)S(1)} %get-tuple-element.28.refs_5_), channel_id=1, source_target_pairs={{4,0},{5,1},{6,2},{7,3},{8,12},{9,13},{10,14},{11,15},{20,16},{21,... | collective-permute-start | bytes 786440 | tf_op jit(solution)/shard_map/ppermute | solution.py:64
  63.1 4.0 %shard_map.88 = (bf16[4,1024,128]{2,1,0:T(8,128)(2,1)S(1)}, s32[4,2,9]{2,1,0:T(2,128)S(1)}, f32[4,1024,128]{2,1,0:T(8,128)S(1)}, f32[4,1024,128]{2,1,0:T(8,128)S(1)}, f32[4,1024,128]{2,1,0:T(8,128)S(1)}) custom-call(s32[16]{0:T(128)S(1)} %copy-done.3, s32[2,8]{1,0:T(2,128)S(1)} %pad_add_fusion.2.list_ref, bf16[128,4096]{1,0:T(8,128)(2,1)S(1)} %copy-done, ...), custom_call_target="tpu_custom_call" | custom-call | flops 268435456 | bytes 4194304 | tf_op jit(solution)/shard_map/pallas_call | solution.py:334
  67.1 2.0 %shard_map.89 = (bf16[2,128,512]{2,1,0:T(8,128)(2,1)S(1)}, bf16[2,128,512]{2,1,0:T(8,128)(2,1)S(1)}, bf16[2,128,512]{2,1,0:T(8,128)(2,1)S(1)}) custom-call(s32[16]{0:T(128)S(1)} %copy-done.3, s32[2,8]{1,0:T(2,128)S(1)} %pad_add_fusion.3.refs_0_, s32[2,8]{1,0:T(2,128)S(1)} %pad_add_fusion.4.refs_1_, s32[2,8]{1,0:T(2,128)S(1)} %pad_add_fusion.5.refs_0_.refs_2_, ...), custom_call_target="tpu_custom_call" | custom-call | bytes 1572864 | tf_op jit(solution)/shard_map/pallas_call | solution.py:103
  69.1 8.4 %collective-permute-done.19.refs_6_ = bf16[2,128,512]{2,1,0:T(8,128)(2,1)S(1)} collective-permute-done((bf16[2,128,512]{2,1,0:T(8,128)(2,1)S(1)}, bf16[2,128,512]{2,1,0:T(8,128)(2,1)S(1)}, u32[]{:S(2)}, u32[]{:S(2)}) %collective-permute-start.19) | collective-permute-done | bytes 262176 | tf_op jit(solution)/shard_map/ppermute | solution.py:64
  77.5 3.2 %collective-permute-start.22 = (bf16[2,128,512]{2,1,0:T(8,128)(2,1)S(1)}, bf16[2,128,512]{2,1,0:T(8,128)(2,1)S(1)}, u32[]{:S(2)}, u32[]{:S(2)}) collective-permute-start(bf16[2,128,512]{2,1,0:T(8,128)(2,1)S(1)} %get-tuple-element.45), channel_id=1, source_target_pairs={{4,6},{5,7},{6,4},{7,5},{8,10},{9,11},{10,8},{11,9},{20,22},{21,23... | collective-permute-start | bytes 786440 | tf_op jit(solution)/shard_map/ppermute | solution.py:64
  83.3 13.1 %shard_map.90 = (f32[4,1024,128]{2,1,0:T(8,128)S(1)}, f32[4,1024,128]{2,1,0:T(8,128)S(1)}, f32[4,1024,128]{2,1,0:T(8,128)S(1)}) custom-call(s32[16]{0:T(128)S(1)} %copy-done.3, s32[2,8]{1,0:T(2,128)S(1)} %pad_add_fusion.2.list_ref, bf16[4,1024,128]{2,1,0:T(8,128)(2,1)S(1)} %get-tuple-element.29.refs_0_, ...), custom_call_target="tpu_custom_call" | custom-call | flops 1073741824 | bytes 4194304 | tf_op jit(solution)/shard_map/pallas_call | solution.py:334
  96.4 1.4 %shard_map.91 = (f32[4,1024,128]{2,1,0:T(8,128)S(1)}, f32[4,1024,128]{2,1,0:T(8,128)S(1)}, f32[4,1024,128]{2,1,0:T(8,128)S(1)}) custom-call(s32[16]{0:T(128)S(1)} %copy-done.3, s32[2,8]{1,0:T(2,128)S(1)} %pad_add_fusion.2.list_ref, bf16[4,1024,128]{2,1,0:T(8,128)(2,1)S(1)} %get-tuple-element.29.refs_0_, f32[4,1024,128]{2,1,0:T(8,128)S(1)} %get-tuple-element.37.refs_1_, ...), custom_call_target="tpu_custom_call" | custom-call | flops 268435456 | bytes 4194304 | tf_op jit(solution)/shard_map/pallas_call | solution.py:334
  97.8 3.6 %shard_map.92 = bf16[2,128,2048]{2,1,0:T(8,128)(2,1)S(1)} custom-call(s32[16]{0:T(128)S(1)} %copy-done.3, s32[2,8]{1,0:T(2,128)S(1)} %pad_add_fusion.2.list_ref, bf16[4,1024,128]{2,1,0:T(8,128)(2,1)S(1)} %get-tuple-element.29.refs_0_, f32[4,1024,128]{2,1,0:T(8,128)S(1)} %get-tuple-element.42.refs_1_, f32[4,1024,128]{2,1,0:T(8,128)S(1)} %get-tuple-element.43.refs_2_, ...), custom_call_target="tpu_custom_call" | custom-call | flops 268435456 | bytes 4194304 | tf_op jit(solution)/shard_map/pallas_call | solution.py:334
  101.5 3.0 %collective-permute-start.25 = (bf16[128,2048]{1,0:T(8,128)(2,1)S(1)}, bf16[128,2048]{1,0:T(8,128)(2,1)S(1)}, u32[]{:S(2)}, u32[]{:S(2)}) collective-permute-start(bf16[128,2048]{1,0:T(8,128)(2,1)S(1)} %get-tuple-element.48), channel_id=1, source_target_pairs={{0,1},{1,0},{2,3},{3,2},{4,5},{5,4},{6,7},{7,6},{8,9},{9,8},{10,11... | collective-permute-start | bytes 1572872 | tf_op jit(solution)/shard_map/ppermute | solution.py:64
  106.0 1.3 %fusion = bf16[128,4096]{1,0:T(8,128)(2,1)} fusion(bf16[128,2048]{1,0:T(8,128)(2,1)S(1)} %collective-permute-done.25, bf16[128,2048]{1,0:T(8,128)(2,1)S(1)} %get-tuple-element.47, pred[128]{0:T(512)(128)(4,1)S(1)} %iota_compare_fusion, pred[]{:T(512)S(6)} %eq.6), kind=kLoop, calls=%fused_computation.1 | loop fusion | flops 5242880 | bytes 2097281 | tf_op jit(solution)/shard_map/jit(_where)/select_n | solution.py:433
  (58 shorter events, 9.6 us)
Async XLA Ops:
  0.0 5.8 %copy-start.4 = (s32[1,8]{1,0:T(1,128)S(1)}, s32[1,8]{1,0:T(1,128)}, u32[]{:S(2)}) copy-start(s32[1,8]{1,0:T(1,128)} %param.14) | copy-start | bytes 100
  0.0 7.5 %copy-start.1 = (bf16[128,512]{1,0:T(8,128)(2,1)S(1)}, bf16[128,512]{1,0:T(8,128)(2,1)}, u32[]{:S(2)}) copy-start(bf16[128,512]{1,0:T(8,128)(2,1)} %refs_2_.1) | copy-start | bytes 393220
  0.0 7.5 %copy-start.2 = (bf16[128,512]{1,0:T(8,128)(2,1)S(1)}, bf16[128,512]{1,0:T(8,128)(2,1)}, u32[]{:S(2)}) copy-start(bf16[128,512]{1,0:T(8,128)(2,1)} %refs_3_.1) | copy-start | bytes 393220
  0.0 19.2 %copy-start = (bf16[128,4096]{1,0:T(8,128)(2,1)S(1)}, bf16[128,4096]{1,0:T(8,128)(2,1)}, u32[]{:S(2)}) copy-start(bf16[128,4096]{1,0:T(8,128)(2,1)} %refs_0_.1) | copy-start | bytes 3145732
  1.4 28.0 %copy-start.3 = (s32[16]{0:T(128)S(1)}, s32[16]{0:T(128)}, u32[]{:S(2)}) copy-start(s32[16]{0:T(128)} %owner_ref.21) | copy-start | bytes 196
  1.4 29.4 %collective-permute-start.7 = (bf16[512,512]{1,0:T(8,128)(2,1)S(1)}, bf16[512,512]{1,0:T(8,128)(2,1)S(1)}, u32[]{:S(2)}, u32[]{:S(2)}) collective-permute-start(bf16[512,512]{1,0:T(8,128)(2,1)S(1)} %pad_maximum_fusion.refs_3_), channel_id=1, source_target_pairs={{4,8},{5,9},{6,10},{7,11},{8,4},{9,5},{10,6},{11,7},{20,24},{21,25... | collective-permute-start | bytes 1572872 | tf_op jit(solution)/shard_map/ppermute | solution.py:64
  4.7 21.5 %collective-permute-start.5 = (bf16[512,512]{1,0:T(8,128)(2,1)S(1)}, bf16[512,512]{1,0:T(8,128)(2,1)S(1)}, u32[]{:S(2)}, u32[]{:S(2)}) collective-permute-start(bf16[512,512]{1,0:T(8,128)(2,1)S(1)} %pad_maximum_fusion.refs_3_), channel_id=1, source_target_pairs={{0,4},{1,5},{2,6},{3,7},{4,0},{5,1},{6,2},{7,3},{8,12},{9,13},{10,... | collective-permute-start | bytes 1572872 | tf_op jit(solution)/shard_map/ppermute | solution.py:64
  4.8 19.3 %collective-permute-start.8 = (bf16[512,512]{1,0:T(8,128)(2,1)S(1)}, bf16[512,512]{1,0:T(8,128)(2,1)S(1)}, u32[]{:S(2)}, u32[]{:S(2)}) collective-permute-start(bf16[512,512]{1,0:T(8,128)(2,1)S(1)} %pad_maximum_fusion.1), channel_id=1, source_target_pairs={{0,1},{1,0},{2,3},{3,2},{4,5},{5,4},{6,7},{7,6},{8,9},{9,8},{10,11... | collective-permute-start | bytes 1572872 | tf_op jit(solution)/shard_map/ppermute | solution.py:64
  5.8 11.5 %collective-permute-start = (s32[1,8]{1,0:T(1,128)S(1)}, s32[1,8]{1,0:T(1,128)S(1)}, u32[]{:S(2)}, u32[]{:S(2)}) collective-permute-start(s32[1,8]{1,0:T(1,128)S(1)} %copy-done.4), channel_id=1, source_target_pairs={{0,4},{1,5},{2,6},{3,7},{4,0},{5,1},{6,2},{7,3},{8,12},{9,13},{10,... | collective-permute-start | bytes 104 | tf_op jit(solution)/shard_map/ppermute | solution.py:64
  7.6 16.5 %collective-permute-start.3 = (bf16[128,512]{1,0:T(8,128)(2,1)S(1)}, bf16[128,512]{1,0:T(8,128)(2,1)S(1)}, u32[]{:S(2)}, u32[]{:S(2)}) collective-permute-start(bf16[128,512]{1,0:T(8,128)(2,1)S(1)} %pad_maximum_fusion.2), channel_id=1, source_target_pairs={{0,1},{1,0},{2,3},{3,2},{4,5},{5,4},{6,7},{7,6},{8,9},{9,8},{10,11... | collective-permute-start | bytes 393224 | tf_op jit(solution)/shard_map/ppermute | solution.py:64
  17.3 2.8 %collective-permute-start.1 = (s32[2,8]{1,0:T(2,128)S(1)}, s32[2,8]{1,0:T(2,128)S(1)}, u32[]{:S(2)}, u32[]{:S(2)}) collective-permute-start(s32[2,8]{1,0:T(2,128)S(1)} %pad_add_fusion.1), channel_id=1, source_target_pairs={{0,1},{1,0},{2,3},{3,2},{4,5},{5,4},{6,7},{7,6},{8,9},{9,8},{10,11... | collective-permute-start | bytes 200 | tf_op jit(solution)/shard_map/ppermute | solution.py:64
  20.1 2.5 %collective-permute-start.4 = (s32[4,8]{1,0:T(4,128)S(1)}, s32[4,8]{1,0:T(4,128)S(1)}, u32[]{:S(2)}, u32[]{:S(2)}) collective-permute-start(s32[4,8]{1,0:T(4,128)S(1)} %pad_add_fusion), channel_id=1, source_target_pairs={{0,2},{1,3},{2,0},{3,1},{4,6},{5,7},{6,4},{7,5},{8,10},{9,11},{10,... | collective-permute-start | bytes 392 | tf_op jit(solution)/shard_map/ppermute | solution.py:64
  22.6 10.1 %collective-permute-start.2 = (bf16[128,2048]{1,0:T(8,128)(2,1)S(1)}, bf16[128,2048]{1,0:T(8,128)(2,1)S(1)}, u32[]{:S(2)}, u32[]{:S(2)}) collective-permute-start(bf16[128,2048]{1,0:T(8,128)(2,1)S(1)} %slice_select_fusion), channel_id=1, source_target_pairs={{0,1},{1,0},{2,3},{3,2},{4,5},{5,4},{6,7},{7,6},{8,9},{9,8},{10,11... | collective-permute-start | bytes 1572872 | tf_op jit(solution)/shard_map/ppermute | solution.py:64
  24.1 13.5 %collective-permute-start.10 = (bf16[512,512]{1,0:T(8,128)(2,1)S(1)}, bf16[512,512]{1,0:T(8,128)(2,1)S(1)}, u32[]{:S(2)}, u32[]{:S(2)}) collective-permute-start(bf16[512,512]{1,0:T(8,128)(2,1)S(1)} %collective-permute-done.8), channel_id=1, source_target_pairs={{0,4},{1,5},{2,6},{3,7},{4,0},{5,1},{6,2},{7,3},{8,12},{9,13},{10,... | collective-permute-start | bytes 1572872 | tf_op jit(solution)/shard_map/ppermute | solution.py:64
  24.1 15.3 %collective-permute-start.9 = (bf16[512,512]{1,0:T(8,128)(2,1)S(1)}, bf16[512,512]{1,0:T(8,128)(2,1)S(1)}, u32[]{:S(2)}, u32[]{:S(2)}) collective-permute-start(bf16[512,512]{1,0:T(8,128)(2,1)S(1)} %collective-permute-done.8), channel_id=1, source_target_pairs={{4,8},{5,9},{6,10},{7,11},{8,4},{9,5},{10,6},{11,7},{20,24},{21,25... | collective-permute-start | bytes 1572872 | tf_op jit(solution)/shard_map/ppermute | solution.py:64
  26.2 24.2 %collective-permute-start.6 = (bf16[512,512]{1,0:T(8,128)(2,1)S(1)}, bf16[512,512]{1,0:T(8,128)(2,1)S(1)}, u32[]{:S(2)}, u32[]{:S(2)}) collective-permute-start(bf16[512,512]{1,0:T(8,128)(2,1)S(1)} %collective-permute-done.5), channel_id=1, source_target_pairs={{4,8},{5,9},{6,10},{7,11},{8,4},{9,5},{10,6},{11,7},{20,24},{21,25... | collective-permute-start | bytes 1572872 | tf_op jit(solution)/shard_map/ppermute | solution.py:64
  30.8 19.8 %collective-permute-start.11 = (bf16[4,128,512]{2,1,0:T(8,128)(2,1)S(1)}, bf16[4,128,512]{2,1,0:T(8,128)(2,1)S(1)}, u32[]{:S(2)}, u32[]{:S(2)}) collective-permute-start(bf16[4,128,512]{2,1,0:T(8,128)(2,1)S(1)} %shard_map.82.refs_3_), channel_id=1, source_target_pairs={{0,2},{1,3},{2,0},{3,1},{4,6},{5,7},{6,4},{7,5},{8,10},{9,11},{10,... | collective-permute-start | bytes 1572872 | tf_op jit(solution)/shard_map/ppermute | solution.py:64
  32.7 11.8 %collective-permute-start.14 = (bf16[2,128,512]{2,1,0:T(8,128)(2,1)S(1)}, bf16[2,128,512]{2,1,0:T(8,128)(2,1)S(1)}, u32[]{:S(2)}, u32[]{:S(2)}) collective-permute-start(bf16[2,128,512]{2,1,0:T(8,128)(2,1)S(1)} %get-tuple-element.26.refs_3_), channel_id=1, source_target_pairs={{4,0},{5,1},{6,2},{7,3},{8,12},{9,13},{10,14},{11,15},{20,16},{21,... | collective-permute-start | bytes 786440 | tf_op jit(solution)/shard_map/ppermute | solution.py:64
  37.5 9.6 %collective-permute-start.16 = (bf16[2,128,512]{2,1,0:T(8,128)(2,1)S(1)}, bf16[2,128,512]{2,1,0:T(8,128)(2,1)S(1)}, u32[]{:S(2)}, u32[]{:S(2)}) collective-permute-start(bf16[2,128,512]{2,1,0:T(8,128)(2,1)S(1)} %get-tuple-element.34), channel_id=1, source_target_pairs={{4,2},{5,3},{6,0},{7,1},{8,14},{9,15},{10,12},{11,13},{20,18},{21,... | collective-permute-start | bytes 786440 | tf_op jit(solution)/shard_map/ppermute | solution.py:64
  39.4 22.4 %collective-permute-start.18 = (bf16[512,512]{1,0:T(8,128)(2,1)S(1)}, bf16[512,512]{1,0:T(8,128)(2,1)S(1)}, u32[]{:S(2)}, u32[]{:S(2)}) collective-permute-start(bf16[512,512]{1,0:T(8,128)(2,1)S(1)} %collective-permute-done.10), channel_id=1, source_target_pairs={{4,8},{5,9},{6,10},{7,11},{8,4},{9,5},{10,6},{11,7},{20,24},{21,25... | collective-permute-start | bytes 1572872 | tf_op jit(solution)/shard_map/ppermute | solution.py:64
  44.4 10.0 %collective-permute-start.15 = (bf16[2,128,512]{2,1,0:T(8,128)(2,1)S(1)}, bf16[2,128,512]{2,1,0:T(8,128)(2,1)S(1)}, u32[]{:S(2)}, u32[]{:S(2)}) collective-permute-start(bf16[2,128,512]{2,1,0:T(8,128)(2,1)S(1)} %get-tuple-element.27.refs_3_), channel_id=1, source_target_pairs={{4,0},{5,1},{6,2},{7,3},{8,12},{9,13},{10,14},{11,15},{20,16},{21,... | collective-permute-start | bytes 786440 | tf_op jit(solution)/shard_map/ppermute | solution.py:64
  47.2 33.5 %collective-permute-start.13 = (bf16[4,128,512]{2,1,0:T(8,128)(2,1)S(1)}, bf16[4,128,512]{2,1,0:T(8,128)(2,1)S(1)}, u32[]{:S(2)}, u32[]{:S(2)}) collective-permute-start(bf16[4,128,512]{2,1,0:T(8,128)(2,1)S(1)} %shard_map.86.refs_4_), channel_id=1, source_target_pairs={{4,6},{5,7},{6,4},{7,5},{8,10},{9,11},{10,8},{11,9},{20,22},{21,23... | collective-permute-start | bytes 1572872 | tf_op jit(solution)/shard_map/ppermute | solution.py:64
  50.4 31.6 %collective-permute-start.12 = (bf16[4,128,512]{2,1,0:T(8,128)(2,1)S(1)}, bf16[4,128,512]{2,1,0:T(8,128)(2,1)S(1)}, u32[]{:S(2)}, u32[]{:S(2)}) collective-permute-start(bf16[4,128,512]{2,1,0:T(8,128)(2,1)S(1)} %shard_map.84.refs_3_), channel_id=1, source_target_pairs={{0,2},{1,3},{2,0},{3,1},{4,6},{5,7},{6,4},{7,5},{8,10},{9,11},{10,... | collective-permute-start | bytes 1572872 | tf_op jit(solution)/shard_map/ppermute | solution.py:64
  50.6 7.1 %collective-permute-start.17 = (bf16[2,128,512]{2,1,0:T(8,128)(2,1)S(1)}, bf16[2,128,512]{2,1,0:T(8,128)(2,1)S(1)}, u32[]{:S(2)}, u32[]{:S(2)}) collective-permute-start(bf16[2,128,512]{2,1,0:T(8,128)(2,1)S(1)} %get-tuple-element.35), channel_id=1, source_target_pairs={{4,2},{5,3},{6,0},{7,1},{8,14},{9,15},{10,12},{11,13},{20,18},{21,... | collective-permute-start | bytes 786440 | tf_op jit(solution)/shard_map/ppermute | solution.py:64
  54.4 23.1 %collective-permute-start.19 = (bf16[2,128,512]{2,1,0:T(8,128)(2,1)S(1)}, bf16[2,128,512]{2,1,0:T(8,128)(2,1)S(1)}, u32[]{:S(2)}, u32[]{:S(2)}) collective-permute-start(bf16[2,128,512]{2,1,0:T(8,128)(2,1)S(1)} %get-tuple-element.40), channel_id=1, source_target_pairs={{4,6},{5,7},{6,4},{7,5},{8,10},{9,11},{10,8},{11,9},{20,22},{21,23... | collective-permute-start | bytes 786440 | tf_op jit(solution)/shard_map/ppermute | solution.py:64
  57.8 38.6 %collective-permute-start.20 = (bf16[2,128,512]{2,1,0:T(8,128)(2,1)S(1)}, bf16[2,128,512]{2,1,0:T(8,128)(2,1)S(1)}, u32[]{:S(2)}, u32[]{:S(2)}) collective-permute-start(bf16[2,128,512]{2,1,0:T(8,128)(2,1)S(1)} %get-tuple-element.28.refs_5_), channel_id=1, source_target_pairs={{4,0},{5,1},{6,2},{7,3},{8,12},{9,13},{10,14},{11,15},{20,16},{21,... | collective-permute-start | bytes 786440 | tf_op jit(solution)/shard_map/ppermute | solution.py:64
  61.8 34.6 %collective-permute-start.21 = (bf16[2,128,512]{2,1,0:T(8,128)(2,1)S(1)}, bf16[2,128,512]{2,1,0:T(8,128)(2,1)S(1)}, u32[]{:S(2)}, u32[]{:S(2)}) collective-permute-start(bf16[2,128,512]{2,1,0:T(8,128)(2,1)S(1)} %get-tuple-element.41), channel_id=1, source_target_pairs={{4,2},{5,3},{6,0},{7,1},{8,14},{9,15},{10,12},{11,13},{20,18},{21,... | collective-permute-start | bytes 786440 | tf_op jit(solution)/shard_map/ppermute | solution.py:64
  77.5 20.3 %collective-permute-start.22 = (bf16[2,128,512]{2,1,0:T(8,128)(2,1)S(1)}, bf16[2,128,512]{2,1,0:T(8,128)(2,1)S(1)}, u32[]{:S(2)}, u32[]{:S(2)}) collective-permute-start(bf16[2,128,512]{2,1,0:T(8,128)(2,1)S(1)} %get-tuple-element.45), channel_id=1, source_target_pairs={{4,6},{5,7},{6,4},{7,5},{8,10},{9,11},{10,8},{11,9},{20,22},{21,23... | collective-permute-start | bytes 786440 | tf_op jit(solution)/shard_map/ppermute | solution.py:64
  80.7 17.1 %collective-permute-start.23 = (bf16[2,128,512]{2,1,0:T(8,128)(2,1)S(1)}, bf16[2,128,512]{2,1,0:T(8,128)(2,1)S(1)}, u32[]{:S(2)}, u32[]{:S(2)}) collective-permute-start(bf16[2,128,512]{2,1,0:T(8,128)(2,1)S(1)} %get-tuple-element.36.refs_18_.refs_9_), channel_id=1, source_target_pairs={{4,0},{5,1},{6,2},{7,3},{8,12},{9,13},{10,14},{11,15},{20,16},{21,... | collective-permute-start | bytes 786440 | tf_op jit(solution)/shard_map/ppermute | solution.py:64
  82.0 15.8 %collective-permute-start.24 = (bf16[2,128,512]{2,1,0:T(8,128)(2,1)S(1)}, bf16[2,128,512]{2,1,0:T(8,128)(2,1)S(1)}, u32[]{:S(2)}, u32[]{:S(2)}) collective-permute-start(bf16[2,128,512]{2,1,0:T(8,128)(2,1)S(1)} %get-tuple-element.46), channel_id=1, source_target_pairs={{4,2},{5,3},{6,0},{7,1},{8,14},{9,15},{10,12},{11,13},{20,18},{21,... | collective-permute-start | bytes 786440 | tf_op jit(solution)/shard_map/ppermute | solution.py:64
  101.5 4.5 %collective-permute-start.25 = (bf16[128,2048]{1,0:T(8,128)(2,1)S(1)}, bf16[128,2048]{1,0:T(8,128)(2,1)S(1)}, u32[]{:S(2)}, u32[]{:S(2)}) collective-permute-start(bf16[128,2048]{1,0:T(8,128)(2,1)S(1)} %get-tuple-element.48), channel_id=1, source_target_pairs={{0,1},{1,0},{2,3},{3,2},{4,5},{5,4},{6,7},{7,6},{8,9},{9,8},{10,11... | collective-permute-start | bytes 1572872 | tf_op jit(solution)/shard_map/ppermute | solution.py:64
